TPU v7x, 128 devices: a whole 4x4x4 slice. The times are simulated.
128 devices in a mesh: slab: 32 (over y, z, core), col: 4 (over x).
Axes of the slice: x: 4, y: 4, z: 4, core: 2. Of those that a mesh axis runs over, the one named last changes fastest.
Arguments:
- input_map: float32 [64, 64, 192, 128], P('col', 'slab'), may hold values from -24 to 24
- output_map: float32 [64, 64, 192, 128], P('col', 'slab'), may hold values from -24 to 24
- region_ids: int32 [64, 192, 128], P('slab'), may hold values from 0 to 7
- region_cond: float32 [8], replicated, may hold values from 0.3 to 3
- shift_ids: int32 [2], replicated, may hold values from 0 to 7
Outputs:
- ctrl_factor: float32 [2, 64, 64, 192, 128], P(None, None, 'slab', 'col')
- obsv_factor: float32 [2, 64, 64, 192, 128], P(None, None, 'slab', 'col')
- cross_gram: float32 [128, 128], P('slab', 'col')
All inputs are finite; a program needn't handle non-finite values.
Results may differ from a plain program's by a relative error of at most 0.000098.
Values sent between devices are 32-bit elements; how exact they have to be, the bound alone decides.
A program may use at most 192 MiB of HBM per device.

v0:
```python
import math

import jax
import jax.numpy as jnp
from jax import lax
from jax.sharding import PartitionSpec as P

ADI = 2
STEPS = 3


def extended(block, sides, width):
    for axis, dim in sides:
        count = lax.axis_size(axis)
        forward = [(i, i + 1) for i in range(count - 1)]
        backward = [(target, source) for source, target in forward]
        low = lax.ppermute(
            lax.slice_in_dim(block, block.shape[dim] - width, None, axis=dim), axis, forward
        )
        high = lax.ppermute(lax.slice_in_dim(block, 0, width, axis=dim), axis, backward)
        block = jnp.concatenate([low, block, high], axis=dim)
    return block


def lookup(region_ids, region_cond):
    summed = jnp.zeros(region_ids.shape, jnp.float32)
    for region in range(region_cond.shape[0]):
        summed = summed + jnp.where(region_ids == region, region_cond[region], jnp.float32(0.0))
    return summed


def conduction(field_in, cond_ext):
    centre = field_in[:, 1:-1]
    cond_mid = cond_ext[1:-1]
    summed = 0.5 * (cond_mid + cond_ext[2:]) * (centre - field_in[:, 2:])
    summed = summed + 0.5 * (cond_mid + cond_ext[:-2]) * (centre - field_in[:, :-2])
    cond_y = jnp.pad(cond_mid, ((0, 0), (1, 1), (0, 0)))
    field_y = jnp.pad(centre, ((0, 0), (0, 0), (1, 1), (0, 0)))
    summed = summed + 0.5 * (cond_mid + cond_y[:, 2:]) * (centre - field_y[:, :, 2:])
    summed = summed + 0.5 * (cond_mid + cond_y[:, :-2]) * (centre - field_y[:, :, :-2])
    cond_z = jnp.pad(cond_mid, ((0, 0), (0, 0), (1, 1)))
    field_z = jnp.pad(centre, ((0, 0), (0, 0), (0, 0), (1, 1)))
    summed = summed + 0.5 * (cond_mid + cond_z[:, :, 2:]) * (centre - field_z[:, :, :, 2:])
    summed = summed + 0.5 * (cond_mid + cond_z[:, :, :-2]) * (centre - field_z[:, :, :, :-2])
    return summed


def bounds(shift_val, cond_max):
    high_eig = shift_val + 12.0 * cond_max
    mid_eig = 0.5 * (high_eig + shift_val)
    half_span = 0.5 * (high_eig - shift_val)
    return (mid_eig, half_span, mid_eig / half_span)


def solve_slabs(right_side, shift_val, cond_max, cond_ext):
    mid_eig, half_span, ratio_eig = bounds(shift_val, cond_max)
    rho_now = 1.0 / ratio_eig
    solution = jnp.zeros_like(right_side)
    residual = right_side
    direction = right_side / mid_eig
    for sweep_idx in range(STEPS - 1):
        solution = solution + direction
        padded = extended(direction, (("slab", 1),), 1)
        applied = conduction(padded, cond_ext) + shift_val * direction
        residual = residual - applied
        rho_next = 1.0 / (2.0 * ratio_eig - rho_now)
        direction = rho_next * rho_now * direction + 2.0 * rho_next / half_span * residual
        rho_now = rho_next
    return solution + direction


def run_segments(stacked, shifts, solver):
    factors = []
    current = stacked
    for segment_idx in range(ADI):
        shift_val = shifts[segment_idx]
        if segment_idx == 0:
            current = solver(stacked, shift_val)
        else:
            current = current - (shifts[segment_idx - 1] + shift_val) * solver(current, shift_val)
        factors.append(jnp.sqrt(2.0 * shift_val) * current)
    return jnp.stack(factors)


def body(input_map, output_map, region_ids, region_cond, shift_ids):
    col_local = input_map.shape[0]
    local_x = input_map.shape[1]
    cond_cells = lookup(region_ids, region_cond)
    cond_max = jnp.max(region_cond)
    shifts = 0.25 * jnp.exp2(shift_ids.astype(jnp.float32))
    total_x = local_x * lax.axis_size("slab")
    stacked = jnp.concatenate([input_map, output_map], 0)
    cond_ext = extended(cond_cells, (("slab", 0),), 1)
    factor_stack = run_segments(
        stacked, shifts, lambda rhs, shift_val: solve_slabs(rhs, shift_val, cond_max, cond_ext)
    )
    ctrl_local = factor_stack[:, :col_local]
    obsv_local = factor_stack[:, col_local:]
    ctrl_cols, obsv_cols = (
        lax.all_to_all(ctrl_local, "col", split_axis=3, concat_axis=1, tiled=True),
        lax.all_to_all(obsv_local, "col", split_axis=3, concat_axis=1, tiled=True),
    )
    row_count = ctrl_cols.shape[0] * ctrl_cols.shape[1]
    ctrl_flat = ctrl_cols.reshape(row_count, -1)
    obsv_flat = obsv_cols.reshape(row_count, -1)
    partial_value = lax.dot_general(
        ctrl_flat,
        obsv_flat,
        (((1,), (1,)), ((), ())),
        precision=lax.Precision.HIGHEST,
        preferred_element_type=jnp.float32,
    )
    cells_total = total_x * region_ids.shape[1] * region_ids.shape[2]
    norm_scale = 1.0 / math.sqrt(cells_total)
    whole_sum = lax.psum(partial_value, ("slab", "col"))
    tile_rows = row_count // lax.axis_size("slab")
    tile_cols = row_count // lax.axis_size("col")
    own_tile = lax.dynamic_slice(
        whole_sum,
        (lax.axis_index("slab") * tile_rows, lax.axis_index("col") * tile_cols),
        (tile_rows, tile_cols),
    )
    return (ctrl_cols, obsv_cols, own_tile * norm_scale)


def solution(mesh):
    placed = (
        P("col", "slab", None, None),
        P("col", "slab", None, None),
        P("slab", None, None),
        P(),
        P(),
    )
    return jax.shard_map(
        body,
        mesh=mesh,
        in_specs=placed,
        out_specs=(
            P(None, None, "slab", "col", None),
            P(None, None, "slab", "col", None),
            P("slab", "col"),
        ),
        check_vma=False,
    )
```

profile of v0, /device:TPU:1, one launch (start us, length us, event | category | flops | bytes accessed | tf_op | source)
XLA Modules:
  0.0 643.6 jit_solution(5252572299411760887)
XLA Ops:
  11.8 3.9 constant_dynamic-update-slice_fusion.1
  17.6 3.2 broadcast_divide_fusion.1
  20.9 3.3 fusion.105
  25.4 3.3 collective-permute-start.1
  28.8 3.5 collective-permute-start.3
  33.0 5.2 select_add_fusion
  44.6 22.0 %collective-permute-done = f32[1,192,128]{2,1,0:T(8,128)S(1)} collective-permute-done((f32[1,192,128]{2,1,0:T(8,128)S(1)}, f32[1,192,128]{2,1,0:T(8,128)S(1)}, u32[]{:S(2)}, u32[]{:S(2)}) %collective-permute-start) | collective-permute-done | bytes 98336 | tf_op jit(solution)/shard_map/ppermute | solution.py:20
  68.0 23.3 %multiply_add_fusion.1 = (f32[32,2,192,128]{3,2,1,0:T(8,128)S(1)}, f32[32,2,192,128]{3,2,1,0:T(8,128)}) fusion(f32[32,2,192,128]{3,2,1,0:T(8,128)} %copy-done.1, f32[]{:T(128)S(6)} %div.53, f32[]{:T(128)S(6)} %mul.354, f32[32,2,192,128]{3,2,1,0:T(8,128)} %constant_dynamic-update-slice_fusion, f32[]{:T(128)} %bitcast, ...), kind=kLoop, calls=%fused_computation.116 | loop fusion | flops 39321600 | bytes 32636940 | tf_op jit(solution)/shard_map/add | solution.py:67
  91.3 3.2 fusion.104
  97.8 4.4 collective-permute-start.5
  103.6 32.0 %collective-permute-done.4 = f32[32,1,192,128]{3,2,1,0:T(8,128)} collective-permute-done((f32[32,1,192,128]{3,2,1,0:T(8,128)}, f32[32,1,192,128]{3,2,1,0:T(8,128)}, u32[]{:S(2)}, u32[]{:S(2)}) %collective-permute-start.4) | collective-permute-done | bytes 3145760 | tf_op jit(solution)/shard_map/ppermute | solution.py:20
  136.7 26.0 %broadcast_divide_fusion = (f32[32,2,192,128]{3,2,1,0:T(8,128)S(1)}, f32[32,2,192,128]{3,2,1,0:T(8,128)}) fusion(f32[]{:T(128)S(6)} %mul.397, f32[32,2,192,128]{3,2,1,0:T(8,128)} %get-tuple-element.8, f32[32,2,192,128]{3,2,1,0:T(8,128)} %copy-done.3, f32[]{:T(128)} %bitcast, f32[2,192,128]{2,1,0:T(8,128)S(1)} %get-tuple-element.29, ...), kind=kLoop, calls=%fused_computation.117 | loop fusion | flops 45613056 | bytes 38928404 | tf_op jit(solution)/shard_map/div | solution.py:60
  162.7 3.8 fusion.103
  169.2 4.4 collective-permute-start.7
  175.1 31.8 %collective-permute-done.6 = f32[32,1,192,128]{3,2,1,0:T(8,128)} collective-permute-done((f32[32,1,192,128]{3,2,1,0:T(8,128)}, f32[32,1,192,128]{3,2,1,0:T(8,128)}, u32[]{:S(2)}, u32[]{:S(2)}) %collective-permute-start.6) | collective-permute-done | bytes 3145760 | tf_op jit(solution)/shard_map/ppermute | solution.py:20
  208.1 26.6 %multiply_add_fusion = (f32[32,2,192,128]{3,2,1,0:T(8,128)S(1)}, f32[32,2,192,128]{3,2,1,0:T(8,128)}, f32[1,32,2,192,128]{4,3,2,1,0:T(8,128)}) fusion(f32[]{:T(128)S(6)} %div.61, f32[]{:T(128)S(6)} %mul.400, f32[32,2,192,128]{3,2,1,0:T(8,128)} %get-tuple-element.6, f32[]{:T(128)S(6)} %mul.397, f32[32,2,192,128]{3,2,1,0:T(8,128)} %copy-done.2, f32[]{:T(128)} %bitcast.10, ...), kind=kLoop, calls=%fused_computation.114 | loop fusion | flops 42467328 | bytes 38928404 | tf_op jit(solution)/shard_map/add | solution.py:67
  234.7 3.8 fusion.102
  241.2 4.6 collective-permute-start.9
  247.8 31.1 %collective-permute-done.8 = f32[32,1,192,128]{3,2,1,0:T(8,128)} collective-permute-done((f32[32,1,192,128]{3,2,1,0:T(8,128)}, f32[32,1,192,128]{3,2,1,0:T(8,128)}, u32[]{:S(2)}, u32[]{:S(2)}) %collective-permute-start.8) | collective-permute-done | bytes 3145760 | tf_op jit(solution)/shard_map/ppermute | solution.py:20
  280.1 27.0 %fusion.47 = f32[1,32,2,192,128]{4,3,2,1,0:T(8,128)S(1)} fusion(f32[32,2,192,128]{3,2,1,0:T(8,128)} %get-tuple-element.6, f32[32,2,192,128]{3,2,1,0:T(8,128)} %get-tuple-element.4, f32[32,2,192,128]{3,2,1,0:T(8,128)} %copy-done, f32[32,1,192,128]{3,2,1,0:T(8,128)} %collective-permute-done.9, f32[32,1,192,128]{3,2,1,0:T(8,128)} %collective-permute-done.8, ...), kind=kLoop, calls=%fused_computation.65 | loop fusion | flops 48758784 | bytes 32636952 | tf_op jit(solution)/shard_map/stack | solution.py:82
  310.3 7.6 %copy.32 = f32[2,16,2,192,128]{4,2,1,0,3:T(2,128)} copy(f32[2,16,2,192,128]{4,3,2,1,0:T(8,128)S(1)} %get-tuple-element.10) | data formatting | bytes 12582912 | tf_op jit(solution)/shard_map/slice | solution.py:97
  317.9 5.3 all-to-all-start
  323.1 10.2 %copy.34 = f32[2,16,2,192,128]{4,2,1,0,3:T(2,128)} copy(f32[2,16,2,192,128]{4,3,2,1,0:T(8,128)} %get-tuple-element.9) | data formatting | bytes 12582912 | tf_op jit(solution)/shard_map/slice | solution.py:98
  333.4 51.1 %all-to-all-done = f32[2,16,2,192,128]{4,2,1,0,3:T(2,128)} async-done(((f32[2,16,2,192,128]{4,2,1,0,3:T(2,128)}), f32[2,16,2,192,128]{4,2,1,0,3:T(2,128)}, u32[]{:S(2)}, u32[]{:S(2)}) %all-to-all-start) | async-done | bytes 6291488 | tf_op jit(solution)/shard_map/all_to_all | solution.py:100
  384.5 5.2 all-to-all-start.1
  390.0 9.0 %copy.41 = f32[2,16,2,4,48,128]{5,4,2,1,3,0:T(8,128)} copy(f32[2,16,2,4,48,128]{5,2,1,0,4,3:T(2,128)} %bitcast.12) | data formatting | bytes 12582912 | tf_op jit(solution)/shard_map/all_to_all | solution.py:100
  399.0 7.5 %reshape.20 = f32[128,12288]{1,0:T(8,128)} reshape(f32[2,4,16,2,48,128]{5,4,3,2,1,0:T(8,128)} %bitcast.32) | data formatting | bytes 12582912 | tf_op jit(solution)/shard_map/reshape | solution.py:104
  406.5 25.3 %all-to-all-done.1 = f32[2,16,2,192,128]{4,2,1,0,3:T(2,128)} async-done(((f32[2,16,2,192,128]{4,2,1,0,3:T(2,128)}), f32[2,16,2,192,128]{4,2,1,0,3:T(2,128)}, u32[]{:S(2)}, u32[]{:S(2)}) %all-to-all-start.1) | async-done | bytes 6291488 | tf_op jit(solution)/shard_map/all_to_all | solution.py:101
  431.7 9.0 %copy.40 = f32[2,16,2,4,48,128]{5,4,2,1,3,0:T(8,128)} copy(f32[2,16,2,4,48,128]{5,2,1,0,4,3:T(2,128)} %bitcast.15) | data formatting | bytes 12582912 | tf_op jit(solution)/shard_map/all_to_all | solution.py:101
  440.8 7.4 %reshape.21 = f32[128,12288]{1,0:T(8,128)} reshape(f32[2,4,16,2,48,128]{5,4,3,2,1,0:T(8,128)} %bitcast.34) | data formatting | bytes 12582912 | tf_op jit(solution)/shard_map/reshape | solution.py:105
  448.2 8.8 %fusion.109 = f32[128,128]{1,0:T(8,128)} fusion(f32[128,12288]{1,0:T(8,128)} %reshape.20, f32[128,12288]{1,0:T(8,128)} %reshape.21), kind=kOutput, calls=%fused_computation.151 | convolution fusion | flops 2415919104 | bytes 12648448 | tf_op jit(solution)/shard_map/dot_general | solution.py:106
  457.1 178.4 %all-reduce.12.cloned.1.call-done = f32[128,128]{1,0:T(8,128)} async-done(((f32[128,128]{1,0:T(8,128)}), f32[128,128]{1,0:T(8,128)}) %all-reduce.12.cloned.1.call-update) | async-done | bytes 65552 | tf_op jit(solution)/shard_map/psum | solution.py:115
  (38 shorter events, 30.5 us)
Async XLA Ops:
  7.2 8.6 %copy-start.5 = (f32[16,2,192,128]{3,2,1,0:T(8,128)S(1)}, f32[16,2,192,128]{3,2,1,0:T(8,128)}, u32[]{:S(2)}) copy-start(f32[16,2,192,128]{3,2,1,0:T(8,128)} %param.6) | copy-start | bytes 9437188
  20.9 4.6 copy-start.1
  20.9 11.4 %copy-start.7 = (f32[8]{0:T(128)S(1)}, f32[8]{0:T(128)}, u32[]{:S(2)}) copy-start(f32[8]{0:T(128)} %param.8) | copy-start | bytes 100
  20.9 12.1 %copy-start.6 = (s32[2,192,128]{2,1,0:T(8,128)S(1)}, s32[2,192,128]{2,1,0:T(8,128)}, u32[]{:S(2)}) copy-start(s32[2,192,128]{2,1,0:T(8,128)} %param.7) | copy-start | bytes 589828
  25.4 42.5 %collective-permute-start.1 = (f32[32,1,192,128]{3,2,1,0:T(8,128)}, f32[32,1,192,128]{3,2,1,0:T(8,128)}, u32[]{:S(2)}, u32[]{:S(2)}) collective-permute-start(f32[32,1,192,128]{3,2,1,0:T(8,128)} %get-tuple-element.22), channel_id=1, source_target_pairs={{4,0},{8,4},{12,8},{16,12},{20,16},{24,20},{28,24},{32,28},{36,32}... | collective-permute-start | bytes 9437192 | tf_op jit(solution)/shard_map/ppermute | solution.py:20
  28.8 39.2 %collective-permute-start.3 = (f32[32,1,192,128]{3,2,1,0:T(8,128)}, f32[32,1,192,128]{3,2,1,0:T(8,128)}, u32[]{:S(2)}, u32[]{:S(2)}) collective-permute-start(f32[32,1,192,128]{3,2,1,0:T(8,128)} %get-tuple-element.23), channel_id=1, source_target_pairs={{0,4},{4,8},{8,12},{12,16},{16,20},{20,24},{24,28},{28,32},{32,36}... | collective-permute-start | bytes 9437192 | tf_op jit(solution)/shard_map/ppermute | solution.py:17
  38.2 28.4 %collective-permute-start = (f32[1,192,128]{2,1,0:T(8,128)S(1)}, f32[1,192,128]{2,1,0:T(8,128)S(1)}, u32[]{:S(2)}, u32[]{:S(2)}) collective-permute-start(f32[1,192,128]{2,1,0:T(8,128)S(1)} %get-tuple-element.30), channel_id=1, source_target_pairs={{4,0},{8,4},{12,8},{16,12},{20,16},{24,20},{28,24},{32,28},{36,32}... | collective-permute-start | bytes 294920 | tf_op jit(solution)/shard_map/ppermute | solution.py:20
  40.7 27.1 %collective-permute-start.2 = (f32[1,192,128]{2,1,0:T(8,128)S(1)}, f32[1,192,128]{2,1,0:T(8,128)S(1)}, u32[]{:S(2)}, u32[]{:S(2)}) collective-permute-start(f32[1,192,128]{2,1,0:T(8,128)S(1)} %get-tuple-element.31), channel_id=1, source_target_pairs={{0,4},{4,8},{8,12},{12,16},{16,20},{20,24},{24,28},{28,32},{32,36}... | collective-permute-start | bytes 294920 | tf_op jit(solution)/shard_map/ppermute | solution.py:17
  91.3 4.6 copy-start.3
  95.9 39.6 %collective-permute-start.4 = (f32[32,1,192,128]{3,2,1,0:T(8,128)}, f32[32,1,192,128]{3,2,1,0:T(8,128)}, u32[]{:S(2)}, u32[]{:S(2)}) collective-permute-start(f32[32,1,192,128]{3,2,1,0:T(8,128)} %get-tuple-element.20), channel_id=1, source_target_pairs={{4,0},{8,4},{12,8},{16,12},{20,16},{24,20},{28,24},{32,28},{36,32}... | collective-permute-start | bytes 9437192 | tf_op jit(solution)/shard_map/ppermute | solution.py:20
  97.8 38.9 %collective-permute-start.5 = (f32[32,1,192,128]{3,2,1,0:T(8,128)}, f32[32,1,192,128]{3,2,1,0:T(8,128)}, u32[]{:S(2)}, u32[]{:S(2)}) collective-permute-start(f32[32,1,192,128]{3,2,1,0:T(8,128)} %get-tuple-element.21), channel_id=1, source_target_pairs={{0,4},{4,8},{8,12},{12,16},{16,20},{20,24},{24,28},{28,32},{32,36}... | collective-permute-start | bytes 9437192 | tf_op jit(solution)/shard_map/ppermute | solution.py:17
  162.7 4.6 copy-start.2
  167.3 39.6 %collective-permute-start.6 = (f32[32,1,192,128]{3,2,1,0:T(8,128)}, f32[32,1,192,128]{3,2,1,0:T(8,128)}, u32[]{:S(2)}, u32[]{:S(2)}) collective-permute-start(f32[32,1,192,128]{3,2,1,0:T(8,128)} %get-tuple-element.18), channel_id=1, source_target_pairs={{4,0},{8,4},{12,8},{16,12},{20,16},{24,20},{28,24},{32,28},{36,32}... | collective-permute-start | bytes 9437192 | tf_op jit(solution)/shard_map/ppermute | solution.py:20
  169.2 38.9 %collective-permute-start.7 = (f32[32,1,192,128]{3,2,1,0:T(8,128)}, f32[32,1,192,128]{3,2,1,0:T(8,128)}, u32[]{:S(2)}, u32[]{:S(2)}) collective-permute-start(f32[32,1,192,128]{3,2,1,0:T(8,128)} %get-tuple-element.19), channel_id=1, source_target_pairs={{0,4},{4,8},{8,12},{12,16},{16,20},{20,24},{24,28},{28,32},{32,36}... | collective-permute-start | bytes 9437192 | tf_op jit(solution)/shard_map/ppermute | solution.py:17
  234.7 4.6 copy-start
  239.3 39.6 %collective-permute-start.8 = (f32[32,1,192,128]{3,2,1,0:T(8,128)}, f32[32,1,192,128]{3,2,1,0:T(8,128)}, u32[]{:S(2)}, u32[]{:S(2)}) collective-permute-start(f32[32,1,192,128]{3,2,1,0:T(8,128)} %get-tuple-element.15), channel_id=1, source_target_pairs={{4,0},{8,4},{12,8},{16,12},{20,16},{24,20},{28,24},{32,28},{36,32}... | collective-permute-start | bytes 9437192 | tf_op jit(solution)/shard_map/ppermute | solution.py:20
  241.2 38.9 %collective-permute-start.9 = (f32[32,1,192,128]{3,2,1,0:T(8,128)}, f32[32,1,192,128]{3,2,1,0:T(8,128)}, u32[]{:S(2)}, u32[]{:S(2)}) collective-permute-start(f32[32,1,192,128]{3,2,1,0:T(8,128)} %get-tuple-element.16), channel_id=1, source_target_pairs={{0,4},{4,8},{8,12},{12,16},{16,20},{20,24},{24,28},{28,32},{32,36}... | collective-permute-start | bytes 9437192 | tf_op jit(solution)/shard_map/ppermute | solution.py:17
  280.1 27.0 %copy-start.4 = (f32[1,32,2,192,128]{4,3,2,1,0:T(8,128)S(1)}, f32[1,32,2,192,128]{4,3,2,1,0:T(8,128)}, u32[]{:S(2)}) copy-start(f32[1,32,2,192,128]{4,3,2,1,0:T(8,128)} %get-tuple-element.17) | copy-start | bytes 18874372
  317.9 66.6 %all-to-all-start = ((f32[2,16,2,192,128]{4,2,1,0,3:T(2,128)}), f32[2,16,2,192,128]{4,2,1,0,3:T(2,128)}, u32[]{:S(2)}, u32[]{:S(2)}) async-start(f32[2,16,2,192,128]{4,2,1,0,3:T(2,128)} %copy.32), calls=%async_computation | async-start | bytes 12582912 | tf_op jit(solution)/shard_map/all_to_all | solution.py:100
  384.5 47.3 %all-to-all-start.1 = ((f32[2,16,2,192,128]{4,2,1,0,3:T(2,128)}), f32[2,16,2,192,128]{4,2,1,0,3:T(2,128)}, u32[]{:S(2)}, u32[]{:S(2)}) async-start(f32[2,16,2,192,128]{4,2,1,0,3:T(2,128)} %copy.34), calls=%async_computation.1 | async-start | bytes 12582912 | tf_op jit(solution)/shard_map/all_to_all | solution.py:101
  389.7 245.7 %all-reduce.12.cloned.1.call-start = ((), (), s32[]{:S(2)}) async-start(), calls=%async_computation.2 | async-start | bytes 131072 | tf_op jit(solution)/shard_map/psum | solution.py:115
Sparse Core Ops, SparseCore 0:
  457.2 178.1 all-reduce.11
where the time goes:
time: 645 us; the launch traced here: 644 us
  waiting for transfers between devices  376 us (58%)
  other arithmetic  118 us (18%)
  local copies, waits for them, and re-layouts  76.2 us (12%)
  starting transfers between devices  42.3 us (7%)
  between operations  21.9 us (3%)
  matrix products  8.8 us (1%)
    psum x1, waiting for transfers between devices, body(): whole_sum = lax.psum(partial_value, ('slab', 'col'))  178 us
    ppermute x5, waiting for transfers between devices, extended(): lax.ppermute(lax.slice_in_dim(block, 0, width, axis=dim), axis, backward)  117 us
    all_to_all x1, waiting for transfers between devices, body(): lax.all_to_all(ctrl_local, 'col', split_axis=3, concat_axis=1, tiled=True)  51.1 us
    add x2, other arithmetic, solve_slabs(): rho_next * rho_now * direction + 2.0 * rho_next / half_span * residual  49.9 us
    another operation x2, other arithmetic, run_segments(): return jnp.stack(factors)  30.2 us
    div x2, other arithmetic, solve_slabs(): direction = right_side / mid_eig  29.2 us
    all_to_all x1, waiting for transfers between devices, body(): lax.all_to_all(obsv_local, 'col', split_axis=3, concat_axis=1, tiled=True)  25.3 us
    ppermute x5, starting transfers between devices, extended(): lax.ppermute(lax.slice_in_dim(block, block.shape[dim] - width, None, axis...  19.9 us
  transfers between devices with their start and end apart: 13, of which 11 were waited for; matrix products, arithmetic and copies ran while one was open for 5% of the time, Pallas kernels for 0%

commit v1 on v0

--- a/solution.py
+++ b/solution.py
@@ -112,14 +112,14 @@
     )
     cells_total = total_x * region_ids.shape[1] * region_ids.shape[2]
     norm_scale = 1.0 / math.sqrt(cells_total)
-    whole_sum = lax.psum(partial_value, ("slab", "col"))
-    tile_rows = row_count // lax.axis_size("slab")
-    tile_cols = row_count // lax.axis_size("col")
-    own_tile = lax.dynamic_slice(
-        whole_sum,
-        (lax.axis_index("slab") * tile_rows, lax.axis_index("col") * tile_cols),
-        (tile_rows, tile_cols),
-    )
+    slab_count = lax.axis_size("slab")
+    col_count = lax.axis_size("col")
+    tile_rows = row_count // slab_count
+    tile_cols = row_count // col_count
+    tiles = partial_value.reshape(slab_count, tile_rows, col_count, tile_cols)
+    tiles = tiles.transpose(0, 2, 1, 3).reshape(slab_count * col_count, tile_rows, tile_cols)
+    received = lax.all_to_all(tiles, ("slab", "col"), 0, 0, tiled=True)
+    own_tile = jnp.sum(received, axis=0)
     return (ctrl_cols, obsv_cols, own_tile * norm_scale)
 
 

time: 645 us -> 532 us (0.82); the launches traced: 644 us -> 524 us
  waiting for transfers between devices: 376 us -> 197 us
  blocking collectives: 0 us -> 58.5 us
  between operations: 21.9 us -> 9.05 us
  matrix products: 8.8 us -> 20.5 us
    psum x1 -> x0, waiting for transfers between devices: 178 us -> none  [body(): whole_sum = lax.psum(partial_value, ('slab', 'col'))]
    all_to_all x0 -> x1, blocking collectives: none -> 58.5 us  [body(): received = lax.all_to_all(tiles, ('slab', 'col'), 0, 0, tiled=True)]
    dot_general x0 -> x2, local copies, waits for them, and re-layouts: none -> 16 us  [body(): lax.dot_general(ctrl_flat, obsv_flat, (((1,), (1,)), ((), ())), precision...]
    reshape x2 -> x1, local copies, waits for them, and re-layouts: 14.9 us -> 0.17 us  [body(): tiles.transpose(0, 2, 1, 3)]
    dot_general x1, matrix products: 8.8 us -> 20.5 us  [body(): lax.dot_general(ctrl_flat, obsv_flat, (((1,), (1,)), ((), ())), precision...]
  transfers between devices with their start and end apart: 13 -> 12, of which waited for: 11 -> 10; matrix products, arithmetic and copies ran while one was open for 5% -> 6% of each run, Pallas kernels for 0% -> 0%
where the time goes in v1:
time: 532 us; the launch traced here: 524 us
  waiting for transfers between devices  197 us (37%)
  other arithmetic  118 us (22%)
  local copies, waits for them, and re-layouts  78.5 us (15%)
  blocking collectives  58.5 us (11%)
  starting transfers between devices  42.5 us (8%)
  matrix products  20.5 us (4%)
  between operations  9.05 us (2%)
    ppermute x5, waiting for transfers between devices, extended(): lax.ppermute(lax.slice_in_dim(block, 0, width, axis=dim), axis, backward)  117 us
    all_to_all x1, blocking collectives, body(): received = lax.all_to_all(tiles, ('slab', 'col'), 0, 0, tiled=True)  58.5 us
    all_to_all x1, waiting for transfers between devices, body(): lax.all_to_all(ctrl_local, 'col', split_axis=3, concat_axis=1, tiled=True)  50.9 us
    add x2, other arithmetic, solve_slabs(): rho_next * rho_now * direction + 2.0 * rho_next / half_span * residual  49.9 us
    another operation x2, other arithmetic, run_segments(): return jnp.stack(factors)  30.2 us
    div x2, other arithmetic, solve_slabs(): direction = right_side / mid_eig  29.1 us
    all_to_all x1, waiting for transfers between devices, body(): lax.all_to_all(obsv_local, 'col', split_axis=3, concat_axis=1, tiled=True)  24.5 us
    dot_general x1, matrix products, body(): lax.dot_general(ctrl_flat, obsv_flat, (((1,), (1,)), ((), ())), precision...  20.5 us
  transfers between devices with their start and end apart: 12, of which 10 were waited for; matrix products, arithmetic and copies ran while one was open for 6% of the time, Pallas kernels for 0%

profile of v1, /device:TPU:1, one launch (start us, length us, event | category | flops | bytes accessed | tf_op | source)
XLA Modules:
  0.0 523.7 jit_solution(5548097822737255707)
XLA Ops:
  5.3 3.9 constant_dynamic-update-slice_fusion.1
  11.1 3.2 broadcast_divide_fusion.1
  14.4 3.3 fusion.110
  18.9 3.3 collective-permute-start.1
  22.3 3.5 collective-permute-start.3
  26.5 4.9 select_add_fusion
  37.8 22.2 %collective-permute-done = f32[1,192,128]{2,1,0:T(8,128)S(1)} collective-permute-done((f32[1,192,128]{2,1,0:T(8,128)S(1)}, f32[1,192,128]{2,1,0:T(8,128)S(1)}, u32[]{:S(2)}, u32[]{:S(2)}) %collective-permute-start) | collective-permute-done | bytes 98336 | tf_op jit(solution)/shard_map/ppermute | solution.py:20
  61.5 23.3 %multiply_add_fusion.1 = (f32[32,2,192,128]{3,2,1,0:T(8,128)S(1)}, f32[32,2,192,128]{3,2,1,0:T(8,128)}) fusion(f32[32,2,192,128]{3,2,1,0:T(8,128)} %copy-done.1, f32[]{:T(128)S(6)} %div.53, f32[]{:T(128)S(6)} %mul.348, f32[32,2,192,128]{3,2,1,0:T(8,128)} %constant_dynamic-update-slice_fusion, f32[]{:T(128)} %bitcast, ...), kind=kLoop, calls=%fused_computation.118 | loop fusion | flops 39321600 | bytes 32636940 | tf_op jit(solution)/shard_map/add | solution.py:67
  84.8 3.3 fusion.109
  91.3 4.4 collective-permute-start.5
  97.2 31.9 %collective-permute-done.4 = f32[32,1,192,128]{3,2,1,0:T(8,128)} collective-permute-done((f32[32,1,192,128]{3,2,1,0:T(8,128)}, f32[32,1,192,128]{3,2,1,0:T(8,128)}, u32[]{:S(2)}, u32[]{:S(2)}) %collective-permute-start.4) | collective-permute-done | bytes 3145760 | tf_op jit(solution)/shard_map/ppermute | solution.py:20
  130.2 25.9 %broadcast_divide_fusion = (f32[32,2,192,128]{3,2,1,0:T(8,128)S(1)}, f32[32,2,192,128]{3,2,1,0:T(8,128)}) fusion(f32[]{:T(128)S(6)} %mul.391, f32[32,2,192,128]{3,2,1,0:T(8,128)} %get-tuple-element.8, f32[32,2,192,128]{3,2,1,0:T(8,128)} %copy-done.3, f32[]{:T(128)} %bitcast, f32[2,192,128]{2,1,0:T(8,128)S(1)} %get-tuple-element.29, ...), kind=kLoop, calls=%fused_computation.119 | loop fusion | flops 45613056 | bytes 38928404 | tf_op jit(solution)/shard_map/div | solution.py:60
  156.1 3.8 fusion.108
  162.6 4.4 collective-permute-start.7
  168.5 31.8 %collective-permute-done.6 = f32[32,1,192,128]{3,2,1,0:T(8,128)} collective-permute-done((f32[32,1,192,128]{3,2,1,0:T(8,128)}, f32[32,1,192,128]{3,2,1,0:T(8,128)}, u32[]{:S(2)}, u32[]{:S(2)}) %collective-permute-start.6) | collective-permute-done | bytes 3145760 | tf_op jit(solution)/shard_map/ppermute | solution.py:20
  201.5 26.6 %multiply_add_fusion = (f32[32,2,192,128]{3,2,1,0:T(8,128)S(1)}, f32[32,2,192,128]{3,2,1,0:T(8,128)}, f32[1,32,2,192,128]{4,3,2,1,0:T(8,128)}) fusion(f32[]{:T(128)S(6)} %div.61, f32[]{:T(128)S(6)} %mul.394, f32[32,2,192,128]{3,2,1,0:T(8,128)} %get-tuple-element.6, f32[]{:T(128)S(6)} %mul.391, f32[32,2,192,128]{3,2,1,0:T(8,128)} %copy-done.2, f32[]{:T(128)} %bitcast.10, ...), kind=kLoop, calls=%fused_computation.116 | loop fusion | flops 42467328 | bytes 38928404 | tf_op jit(solution)/shard_map/add | solution.py:67
  228.1 3.8 fusion.107
  234.6 4.9 collective-permute-start.9
  241.6 30.7 %collective-permute-done.8 = f32[32,1,192,128]{3,2,1,0:T(8,128)} collective-permute-done((f32[32,1,192,128]{3,2,1,0:T(8,128)}, f32[32,1,192,128]{3,2,1,0:T(8,128)}, u32[]{:S(2)}, u32[]{:S(2)}) %collective-permute-start.8) | collective-permute-done | bytes 3145760 | tf_op jit(solution)/shard_map/ppermute | solution.py:20
  273.5 27.1 %fusion.47 = f32[1,32,2,192,128]{4,3,2,1,0:T(8,128)S(1)} fusion(f32[32,2,192,128]{3,2,1,0:T(8,128)} %get-tuple-element.6, f32[32,2,192,128]{3,2,1,0:T(8,128)} %get-tuple-element.4, f32[32,2,192,128]{3,2,1,0:T(8,128)} %copy-done, f32[32,1,192,128]{3,2,1,0:T(8,128)} %collective-permute-done.9, f32[32,1,192,128]{3,2,1,0:T(8,128)} %collective-permute-done.8, ...), kind=kLoop, calls=%fused_computation.65 | loop fusion | flops 48758784 | bytes 32636952 | tf_op jit(solution)/shard_map/stack | solution.py:82
  303.8 7.6 %copy.28 = f32[2,16,2,192,128]{4,2,1,0,3:T(2,128)} copy(f32[2,16,2,192,128]{4,3,2,1,0:T(8,128)S(1)} %get-tuple-element.10) | data formatting | bytes 12582912 | tf_op jit(solution)/shard_map/slice | solution.py:97
  311.3 5.3 %all-to-all-start = ((f32[2,16,2,192,128]{4,2,1,0,3:T(2,128)}), f32[2,16,2,192,128]{4,2,1,0,3:T(2,128)}, u32[]{:S(2)}, u32[]{:S(2)}) async-start(f32[2,16,2,192,128]{4,2,1,0,3:T(2,128)} %copy.28), calls=%async_computation | async-start | bytes 12582912 | tf_op jit(solution)/shard_map/all_to_all | solution.py:100
  316.6 10.2 %copy.30 = f32[2,16,2,192,128]{4,2,1,0,3:T(2,128)} copy(f32[2,16,2,192,128]{4,3,2,1,0:T(8,128)} %get-tuple-element.9) | data formatting | bytes 12582912 | tf_op jit(solution)/shard_map/slice | solution.py:98
  326.9 50.9 %all-to-all-done = f32[2,16,2,192,128]{4,2,1,0,3:T(2,128)} async-done(((f32[2,16,2,192,128]{4,2,1,0,3:T(2,128)}), f32[2,16,2,192,128]{4,2,1,0,3:T(2,128)}, u32[]{:S(2)}, u32[]{:S(2)}) %all-to-all-start) | async-done | bytes 6291488 | tf_op jit(solution)/shard_map/all_to_all | solution.py:100
  377.7 5.4 %all-to-all-start.1 = ((f32[2,16,2,192,128]{4,2,1,0,3:T(2,128)}), f32[2,16,2,192,128]{4,2,1,0,3:T(2,128)}, u32[]{:S(2)}, u32[]{:S(2)}) async-start(f32[2,16,2,192,128]{4,2,1,0,3:T(2,128)} %copy.30), calls=%async_computation.1 | async-start | bytes 12582912 | tf_op jit(solution)/shard_map/all_to_all | solution.py:101
  383.2 9.0 %copy.47 = f32[2,16,2,4,48,128]{5,4,2,1,3,0:T(8,128)} copy(f32[2,16,2,4,48,128]{5,2,1,0,4,3:T(2,128)} %bitcast.12) | data formatting | bytes 12582912 | tf_op jit(solution)/shard_map/all_to_all | solution.py:100
  392.2 8.5 %dot_general.7 = f32[32,4,12288]{2,1,0:T(4,128)} reshape(f32[2,4,16,2,48,128]{5,4,3,2,1,0:T(8,128)} %bitcast.35) | data formatting | bytes 12582912 | tf_op jit(solution)/shard_map/dot_general | solution.py:106
  400.7 24.5 %all-to-all-done.1 = f32[2,16,2,192,128]{4,2,1,0,3:T(2,128)} async-done(((f32[2,16,2,192,128]{4,2,1,0,3:T(2,128)}), f32[2,16,2,192,128]{4,2,1,0,3:T(2,128)}, u32[]{:S(2)}, u32[]{:S(2)}) %all-to-all-start.1) | async-done | bytes 6291488 | tf_op jit(solution)/shard_map/all_to_all | solution.py:101
  425.2 9.0 %copy.46 = f32[2,16,2,4,48,128]{5,4,2,1,3,0:T(8,128)} copy(f32[2,16,2,4,48,128]{5,2,1,0,4,3:T(2,128)} %bitcast.15) | data formatting | bytes 12582912 | tf_op jit(solution)/shard_map/all_to_all | solution.py:101
  434.2 7.5 %reshape.26 = f32[4,32,12288,1]{2,1,0,3:T(8,128)} reshape(f32[2,4,16,2,48,128]{5,4,3,2,1,0:T(8,128)} %bitcast.37) | data formatting | bytes 12582912 | tf_op jit(solution)/shard_map/dot_general | solution.py:106
  441.7 20.5 %fusion.89 = f32[32,4,4,32]{3,0,1,2:T(8,128)S(1)} fusion(f32[4,32,12288,1]{2,1,0,3:T(8,128)} %reshape.26, f32[32,4,12288,1]{2,1,0,3:T(4,128)} %bitcast.39), kind=kOutput, calls=%fused_computation.121 | convolution fusion | flops 2415919104 | bytes 12648448 | tf_op jit(solution)/shard_map/dot_general | solution.py:106
  462.7 58.5 %all_to_all.41 = f32[128,1,128]{2,1,0:T(1,128)S(1)} all-to-all(f32[128,1,128]{2,1,0:T(1,128)S(1)} %reshape.28), channel_id=1, replica_groups=mesh['slab'=32,'col'=4] {'slab','col'}, dimensions={0} | all-to-all | bytes 131072 | tf_op jit(solution)/shard_map/all_to_all | solution.py:121
  (43 shorter events, 31.6 us)
Async XLA Ops:
  0.6 8.6 %copy-start.5 = (f32[16,2,192,128]{3,2,1,0:T(8,128)S(1)}, f32[16,2,192,128]{3,2,1,0:T(8,128)}, u32[]{:S(2)}) copy-start(f32[16,2,192,128]{3,2,1,0:T(8,128)} %param.6) | copy-start | bytes 9437188
  14.3 4.6 copy-start.1
  14.4 11.4 %copy-start.7 = (f32[8]{0:T(128)S(1)}, f32[8]{0:T(128)}, u32[]{:S(2)}) copy-start(f32[8]{0:T(128)} %param.8) | copy-start | bytes 100
  14.4 12.1 %copy-start.6 = (s32[2,192,128]{2,1,0:T(8,128)S(1)}, s32[2,192,128]{2,1,0:T(8,128)}, u32[]{:S(2)}) copy-start(s32[2,192,128]{2,1,0:T(8,128)} %param.7) | copy-start | bytes 589828
  18.9 42.5 %collective-permute-start.1 = (f32[32,1,192,128]{3,2,1,0:T(8,128)}, f32[32,1,192,128]{3,2,1,0:T(8,128)}, u32[]{:S(2)}, u32[]{:S(2)}) collective-permute-start(f32[32,1,192,128]{3,2,1,0:T(8,128)} %get-tuple-element.22), channel_id=1, source_target_pairs={{4,0},{8,4},{12,8},{16,12},{20,16},{24,20},{28,24},{32,28},{36,32}... | collective-permute-start | bytes 9437192 | tf_op jit(solution)/shard_map/ppermute | solution.py:20
  22.3 39.2 %collective-permute-start.3 = (f32[32,1,192,128]{3,2,1,0:T(8,128)}, f32[32,1,192,128]{3,2,1,0:T(8,128)}, u32[]{:S(2)}, u32[]{:S(2)}) collective-permute-start(f32[32,1,192,128]{3,2,1,0:T(8,128)} %get-tuple-element.23), channel_id=1, source_target_pairs={{0,4},{4,8},{8,12},{12,16},{16,20},{20,24},{24,28},{28,32},{32,36}... | collective-permute-start | bytes 9437192 | tf_op jit(solution)/shard_map/ppermute | solution.py:17
  31.4 28.6 %collective-permute-start = (f32[1,192,128]{2,1,0:T(8,128)S(1)}, f32[1,192,128]{2,1,0:T(8,128)S(1)}, u32[]{:S(2)}, u32[]{:S(2)}) collective-permute-start(f32[1,192,128]{2,1,0:T(8,128)S(1)} %get-tuple-element.30), channel_id=1, source_target_pairs={{4,0},{8,4},{12,8},{16,12},{20,16},{24,20},{28,24},{32,28},{36,32}... | collective-permute-start | bytes 294920 | tf_op jit(solution)/shard_map/ppermute | solution.py:20
  34.0 27.3 %collective-permute-start.2 = (f32[1,192,128]{2,1,0:T(8,128)S(1)}, f32[1,192,128]{2,1,0:T(8,128)S(1)}, u32[]{:S(2)}, u32[]{:S(2)}) collective-permute-start(f32[1,192,128]{2,1,0:T(8,128)S(1)} %get-tuple-element.31), channel_id=1, source_target_pairs={{0,4},{4,8},{8,12},{12,16},{16,20},{20,24},{24,28},{28,32},{32,36}... | collective-permute-start | bytes 294920 | tf_op jit(solution)/shard_map/ppermute | solution.py:17
  84.8 4.6 copy-start.3
  89.4 39.6 %collective-permute-start.4 = (f32[32,1,192,128]{3,2,1,0:T(8,128)}, f32[32,1,192,128]{3,2,1,0:T(8,128)}, u32[]{:S(2)}, u32[]{:S(2)}) collective-permute-start(f32[32,1,192,128]{3,2,1,0:T(8,128)} %get-tuple-element.20), channel_id=1, source_target_pairs={{4,0},{8,4},{12,8},{16,12},{20,16},{24,20},{28,24},{32,28},{36,32}... | collective-permute-start | bytes 9437192 | tf_op jit(solution)/shard_map/ppermute | solution.py:20
  91.3 38.9 %collective-permute-start.5 = (f32[32,1,192,128]{3,2,1,0:T(8,128)}, f32[32,1,192,128]{3,2,1,0:T(8,128)}, u32[]{:S(2)}, u32[]{:S(2)}) collective-permute-start(f32[32,1,192,128]{3,2,1,0:T(8,128)} %get-tuple-element.21), channel_id=1, source_target_pairs={{0,4},{4,8},{8,12},{12,16},{16,20},{20,24},{24,28},{28,32},{32,36}... | collective-permute-start | bytes 9437192 | tf_op jit(solution)/shard_map/ppermute | solution.py:17
  156.1 4.6 copy-start.2
  160.7 39.6 %collective-permute-start.6 = (f32[32,1,192,128]{3,2,1,0:T(8,128)}, f32[32,1,192,128]{3,2,1,0:T(8,128)}, u32[]{:S(2)}, u32[]{:S(2)}) collective-permute-start(f32[32,1,192,128]{3,2,1,0:T(8,128)} %get-tuple-element.18), channel_id=1, source_target_pairs={{4,0},{8,4},{12,8},{16,12},{20,16},{24,20},{28,24},{32,28},{36,32}... | collective-permute-start | bytes 9437192 | tf_op jit(solution)/shard_map/ppermute | solution.py:20
  162.6 38.9 %collective-permute-start.7 = (f32[32,1,192,128]{3,2,1,0:T(8,128)}, f32[32,1,192,128]{3,2,1,0:T(8,128)}, u32[]{:S(2)}, u32[]{:S(2)}) collective-permute-start(f32[32,1,192,128]{3,2,1,0:T(8,128)} %get-tuple-element.19), channel_id=1, source_target_pairs={{0,4},{4,8},{8,12},{12,16},{16,20},{20,24},{24,28},{28,32},{32,36}... | collective-permute-start | bytes 9437192 | tf_op jit(solution)/shard_map/ppermute | solution.py:17
  228.1 4.6 copy-start
  232.7 39.6 %collective-permute-start.8 = (f32[32,1,192,128]{3,2,1,0:T(8,128)}, f32[32,1,192,128]{3,2,1,0:T(8,128)}, u32[]{:S(2)}, u32[]{:S(2)}) collective-permute-start(f32[32,1,192,128]{3,2,1,0:T(8,128)} %get-tuple-element.15), channel_id=1, source_target_pairs={{4,0},{8,4},{12,8},{16,12},{20,16},{24,20},{28,24},{32,28},{36,32}... | collective-permute-start | bytes 9437192 | tf_op jit(solution)/shard_map/ppermute | solution.py:20
  234.6 38.9 %collective-permute-start.9 = (f32[32,1,192,128]{3,2,1,0:T(8,128)}, f32[32,1,192,128]{3,2,1,0:T(8,128)}, u32[]{:S(2)}, u32[]{:S(2)}) collective-permute-start(f32[32,1,192,128]{3,2,1,0:T(8,128)} %get-tuple-element.16), channel_id=1, source_target_pairs={{0,4},{4,8},{8,12},{12,16},{16,20},{20,24},{24,28},{28,32},{32,36}... | collective-permute-start | bytes 9437192 | tf_op jit(solution)/shard_map/ppermute | solution.py:17
  273.5 27.1 %copy-start.4 = (f32[1,32,2,192,128]{4,3,2,1,0:T(8,128)S(1)}, f32[1,32,2,192,128]{4,3,2,1,0:T(8,128)}, u32[]{:S(2)}) copy-start(f32[1,32,2,192,128]{4,3,2,1,0:T(8,128)} %get-tuple-element.17) | copy-start | bytes 18874372
  311.3 66.4 %all-to-all-start = ((f32[2,16,2,192,128]{4,2,1,0,3:T(2,128)}), f32[2,16,2,192,128]{4,2,1,0,3:T(2,128)}, u32[]{:S(2)}, u32[]{:S(2)}) async-start(f32[2,16,2,192,128]{4,2,1,0,3:T(2,128)} %copy.28), calls=%async_computation | async-start | bytes 12582912 | tf_op jit(solution)/shard_map/all_to_all | solution.py:100
  377.7 47.5 %all-to-all-start.1 = ((f32[2,16,2,192,128]{4,2,1,0,3:T(2,128)}), f32[2,16,2,192,128]{4,2,1,0,3:T(2,128)}, u32[]{:S(2)}, u32[]{:S(2)}) async-start(f32[2,16,2,192,128]{4,2,1,0,3:T(2,128)} %copy.30), calls=%async_computation.1 | async-start | bytes 12582912 | tf_op jit(solution)/shard_map/all_to_all | solution.py:101

commit v2 on v1

--- a/solution.py
+++ b/solution.py
@@ -116,10 +116,10 @@
     col_count = lax.axis_size("col")
     tile_rows = row_count // slab_count
     tile_cols = row_count // col_count
-    tiles = partial_value.reshape(slab_count, tile_rows, col_count, tile_cols)
-    tiles = tiles.transpose(0, 2, 1, 3).reshape(slab_count * col_count, tile_rows, tile_cols)
-    received = lax.all_to_all(tiles, ("slab", "col"), 0, 0, tiled=True)
-    own_tile = jnp.sum(received, axis=0)
+    col_parts = partial_value.reshape(row_count, col_count, tile_cols).transpose(1, 0, 2)
+    col_sum = jnp.sum(lax.all_to_all(col_parts, "col", 0, 0, tiled=True), axis=0)
+    row_parts = col_sum.reshape(slab_count, tile_rows, tile_cols)
+    own_tile = jnp.sum(lax.all_to_all(row_parts, "slab", 0, 0, tiled=True), axis=0)
     return (ctrl_cols, obsv_cols, own_tile * norm_scale)
 
 

time: 532 us -> 517 us (0.972); the launches traced: 524 us -> 515 us
  matrix products: 20.5 us -> 8.21 us
    all_to_all x1, waiting for transfers between devices: 24.5 us -> 51 us  [body(): lax.all_to_all(obsv_local, 'col', split_axis=3, concat_axis=1, tiled=True)]
    all_to_all x1, waiting for transfers between devices: 50.9 us -> 25.4 us  [body(): lax.all_to_all(ctrl_local, 'col', split_axis=3, concat_axis=1, tiled=True)]
    dot_general x1, matrix products: 20.5 us -> 8.21 us  [body(): lax.dot_general(ctrl_flat, obsv_flat, (((1,), (1,)), ((), ())), precision...]
    dot_general x2 -> x1, local copies, waits for them, and re-layouts: 16 us -> 7.42 us  [body(): lax.dot_general(ctrl_flat, obsv_flat, (((1,), (1,)), ((), ())), precision...]
    reshape x1, local copies, waits for them, and re-layouts: 0.17 us -> 7.45 us  [body(): ctrl_flat = ctrl_cols.reshape(row_count, -1)]
    all_to_all x1 -> x2, blocking collectives: 58.5 us -> 63.4 us  [the longest x1 56.5 us: body(): lax.all_to_all(row_parts, 'slab', 0, 0, tiled=True)]
where the time goes in v2:
time: 517 us; the launch traced here: 515 us
  waiting for transfers between devices  198 us (38%)
  other arithmetic  118 us (23%)
  local copies, waits for them, and re-layouts  77.1 us (15%)
  blocking collectives  63.4 us (12%)
  starting transfers between devices  42.2 us (8%)
  between operations  8.77 us (2%)
  matrix products  8.21 us (2%)
    ppermute x5, waiting for transfers between devices, extended(): lax.ppermute(lax.slice_in_dim(block, 0, width, axis=dim), axis, backward)  117 us
    all_to_all x1, blocking collectives, body(): lax.all_to_all(row_parts, 'slab', 0, 0, tiled=True)  56.5 us
    all_to_all x1, waiting for transfers between devices, body(): lax.all_to_all(obsv_local, 'col', split_axis=3, concat_axis=1, tiled=True)  51 us
    add x2, other arithmetic, solve_slabs(): rho_next * rho_now * direction + 2.0 * rho_next / half_span * residual  49.9 us
    another operation x2, other arithmetic, run_segments(): return jnp.stack(factors)  30.2 us
    div x2, other arithmetic, solve_slabs(): direction = right_side / mid_eig  29.1 us
    all_to_all x1, waiting for transfers between devices, body(): lax.all_to_all(ctrl_local, 'col', split_axis=3, concat_axis=1, tiled=True)  25.4 us
    ppermute x5, starting transfers between devices, extended(): lax.ppermute(lax.slice_in_dim(block, block.shape[dim] - width, None, axis...  19.9 us
  transfers between devices with their start and end apart: 12, of which 10 were waited for; matrix products, arithmetic and copies ran while one was open for 6% of the time, Pallas kernels for 0%

profile of v2, /device:TPU:1, one launch (start us, length us, event | category | flops | bytes accessed | tf_op | source)
XLA Modules:
  0.0 515.3 jit_solution(2384388008624997984)
XLA Ops:
  5.3 3.9 constant_dynamic-update-slice_fusion.1
  14.4 3.3 fusion.105
  18.9 3.3 collective-permute-start.1
  22.3 3.5 collective-permute-start.3
  26.5 5.0 select_add_fusion
  37.9 22.1 %collective-permute-done = f32[1,192,128]{2,1,0:T(8,128)S(1)} collective-permute-done((f32[1,192,128]{2,1,0:T(8,128)S(1)}, f32[1,192,128]{2,1,0:T(8,128)S(1)}, u32[]{:S(2)}, u32[]{:S(2)}) %collective-permute-start) | collective-permute-done | bytes 98336 | tf_op jit(solution)/shard_map/ppermute | solution.py:20
  61.4 23.3 %multiply_add_fusion.1 = (f32[32,2,192,128]{3,2,1,0:T(8,128)S(1)}, f32[32,2,192,128]{3,2,1,0:T(8,128)}) fusion(f32[32,2,192,128]{3,2,1,0:T(8,128)} %copy-done.1, f32[]{:T(128)S(6)} %div.53, f32[]{:T(128)S(6)} %mul.348, f32[32,2,192,128]{3,2,1,0:T(8,128)} %constant_dynamic-update-slice_fusion, f32[]{:T(128)} %bitcast, ...), kind=kLoop, calls=%fused_computation.116 | loop fusion | flops 39321600 | bytes 32636940 | tf_op jit(solution)/shard_map/add | solution.py:67
  84.8 3.3 fusion.104
  91.3 4.4 collective-permute-start.5
  97.1 31.9 %collective-permute-done.4 = f32[32,1,192,128]{3,2,1,0:T(8,128)} collective-permute-done((f32[32,1,192,128]{3,2,1,0:T(8,128)}, f32[32,1,192,128]{3,2,1,0:T(8,128)}, u32[]{:S(2)}, u32[]{:S(2)}) %collective-permute-start.4) | collective-permute-done | bytes 3145760 | tf_op jit(solution)/shard_map/ppermute | solution.py:20
  130.2 25.9 %broadcast_divide_fusion = (f32[32,2,192,128]{3,2,1,0:T(8,128)S(1)}, f32[32,2,192,128]{3,2,1,0:T(8,128)}) fusion(f32[]{:T(128)S(6)} %mul.391, f32[32,2,192,128]{3,2,1,0:T(8,128)} %get-tuple-element.8, f32[32,2,192,128]{3,2,1,0:T(8,128)} %copy-done.3, f32[]{:T(128)} %bitcast, f32[2,192,128]{2,1,0:T(8,128)S(1)} %get-tuple-element.29, ...), kind=kLoop, calls=%fused_computation.117 | loop fusion | flops 45613056 | bytes 38928404 | tf_op jit(solution)/shard_map/div | solution.py:60
  156.1 3.8 fusion.103
  162.6 4.4 collective-permute-start.7
  168.5 31.8 %collective-permute-done.6 = f32[32,1,192,128]{3,2,1,0:T(8,128)} collective-permute-done((f32[32,1,192,128]{3,2,1,0:T(8,128)}, f32[32,1,192,128]{3,2,1,0:T(8,128)}, u32[]{:S(2)}, u32[]{:S(2)}) %collective-permute-start.6) | collective-permute-done | bytes 3145760 | tf_op jit(solution)/shard_map/ppermute | solution.py:20
  201.5 26.6 %multiply_add_fusion = (f32[32,2,192,128]{3,2,1,0:T(8,128)S(1)}, f32[32,2,192,128]{3,2,1,0:T(8,128)}, f32[1,32,2,192,128]{4,3,2,1,0:T(8,128)}) fusion(f32[]{:T(128)S(6)} %div.61, f32[]{:T(128)S(6)} %mul.394, f32[32,2,192,128]{3,2,1,0:T(8,128)} %get-tuple-element.6, f32[]{:T(128)S(6)} %mul.391, f32[32,2,192,128]{3,2,1,0:T(8,128)} %copy-done.2, f32[]{:T(128)} %bitcast.10, ...), kind=kLoop, calls=%fused_computation.114 | loop fusion | flops 42467328 | bytes 38928404 | tf_op jit(solution)/shard_map/add | solution.py:67
  228.1 3.8 fusion.102
  234.6 4.6 collective-permute-start.9
  241.3 31.0 %collective-permute-done.8 = f32[32,1,192,128]{3,2,1,0:T(8,128)} collective-permute-done((f32[32,1,192,128]{3,2,1,0:T(8,128)}, f32[32,1,192,128]{3,2,1,0:T(8,128)}, u32[]{:S(2)}, u32[]{:S(2)}) %collective-permute-start.8) | collective-permute-done | bytes 3145760 | tf_op jit(solution)/shard_map/ppermute | solution.py:20
  273.5 27.1 %fusion.47 = f32[1,32,2,192,128]{4,3,2,1,0:T(8,128)S(1)} fusion(f32[32,2,192,128]{3,2,1,0:T(8,128)} %get-tuple-element.6, f32[32,2,192,128]{3,2,1,0:T(8,128)} %get-tuple-element.4, f32[32,2,192,128]{3,2,1,0:T(8,128)} %copy-done, f32[32,1,192,128]{3,2,1,0:T(8,128)} %collective-permute-done.9, f32[32,1,192,128]{3,2,1,0:T(8,128)} %collective-permute-done.8, ...), kind=kLoop, calls=%fused_computation.65 | loop fusion | flops 48758784 | bytes 32636952 | tf_op jit(solution)/shard_map/stack | solution.py:82
  303.7 7.5 %copy.35 = f32[2,16,2,192,128]{4,2,1,0,3:T(2,128)} copy(f32[2,16,2,192,128]{4,3,2,1,0:T(8,128)S(1)} %get-tuple-element.9) | data formatting | bytes 12582912 | tf_op jit(solution)/shard_map/slice | solution.py:98
  311.2 5.2 %all-to-all-start.1 = ((f32[2,16,2,192,128]{4,2,1,0,3:T(2,128)}), f32[2,16,2,192,128]{4,2,1,0,3:T(2,128)}, u32[]{:S(2)}, u32[]{:S(2)}) async-start(f32[2,16,2,192,128]{4,2,1,0,3:T(2,128)} %copy.35), calls=%async_computation.1 | async-start | bytes 12582912 | tf_op jit(solution)/shard_map/all_to_all | solution.py:101
  316.5 10.3 %copy.33 = f32[2,16,2,192,128]{4,2,1,0,3:T(2,128)} copy(f32[2,16,2,192,128]{4,3,2,1,0:T(8,128)} %get-tuple-element.10) | data formatting | bytes 12582912 | tf_op jit(solution)/shard_map/slice | solution.py:97
  326.8 51.0 %all-to-all-done.1 = f32[2,16,2,192,128]{4,2,1,0,3:T(2,128)} async-done(((f32[2,16,2,192,128]{4,2,1,0,3:T(2,128)}), f32[2,16,2,192,128]{4,2,1,0,3:T(2,128)}, u32[]{:S(2)}, u32[]{:S(2)}) %all-to-all-start.1) | async-done | bytes 6291488 | tf_op jit(solution)/shard_map/all_to_all | solution.py:101
  377.8 5.5 %all-to-all-start = ((f32[2,16,2,192,128]{4,2,1,0,3:T(2,128)}), f32[2,16,2,192,128]{4,2,1,0,3:T(2,128)}, u32[]{:S(2)}, u32[]{:S(2)}) async-start(f32[2,16,2,192,128]{4,2,1,0,3:T(2,128)} %copy.33), calls=%async_computation | async-start | bytes 12582912 | tf_op jit(solution)/shard_map/all_to_all | solution.py:100
  383.2 9.0 %copy.42 = f32[2,16,2,4,48,128]{5,4,2,1,3,0:T(8,128)} copy(f32[2,16,2,4,48,128]{5,2,1,0,4,3:T(2,128)} %bitcast.15) | data formatting | bytes 12582912 | tf_op jit(solution)/shard_map/all_to_all | solution.py:101
  392.3 7.4 %dot_general.5 = f32[4,32,12288]{2,1,0:T(8,128)} reshape(f32[2,4,16,2,48,128]{5,4,3,2,1,0:T(8,128)} %bitcast.35) | data formatting | bytes 12582912 | tf_op jit(solution)/shard_map/dot_general | solution.py:106
  399.7 25.4 %all-to-all-done = f32[2,16,2,192,128]{4,2,1,0,3:T(2,128)} async-done(((f32[2,16,2,192,128]{4,2,1,0,3:T(2,128)}), f32[2,16,2,192,128]{4,2,1,0,3:T(2,128)}, u32[]{:S(2)}, u32[]{:S(2)}) %all-to-all-start) | async-done | bytes 6291488 | tf_op jit(solution)/shard_map/all_to_all | solution.py:100
  425.1 9.0 %copy.43 = f32[2,16,2,4,48,128]{5,4,2,1,3,0:T(8,128)} copy(f32[2,16,2,4,48,128]{5,2,1,0,4,3:T(2,128)} %bitcast.12) | data formatting | bytes 12582912 | tf_op jit(solution)/shard_map/all_to_all | solution.py:100
  434.1 7.5 %reshape.26 = f32[128,12288,1]{1,0,2:T(8,128)} reshape(f32[2,4,16,2,48,128]{5,4,3,2,1,0:T(8,128)} %bitcast.37) | data formatting | bytes 12582912 | tf_op jit(solution)/shard_map/reshape | solution.py:104
  441.6 8.2 %convolution_bitcast_fusion = f32[4,128,32]{1,2,0:T(8,128)S(1)} fusion(f32[128,12288,1]{1,0,2:T(8,128)} %reshape.26, f32[4,32,12288]{2,1,0:T(8,128)} %dot_general.5), kind=kOutput, calls=%fused_computation.119 | convolution fusion | flops 2415919104 | bytes 12648448 | tf_op jit(solution)/shard_map/dot_general | solution.py:106
  449.8 6.8 %all_to_all.46 = f32[4,128,32]{1,2,0:T(8,128)S(1)} all-to-all(f32[4,128,32]{1,2,0:T(8,128)S(1)} %convolution_bitcast_fusion), channel_id=1, replica_groups=mesh['slab'=32,'col'=4] {'col'}, dimensions={0} | all-to-all | bytes 131072 | tf_op jit(solution)/shard_map/all_to_all | solution.py:120
  456.8 56.5 %all_to_all.47 = f32[32,1,128]{2,1,0:T(1,128)S(1)} all-to-all(f32[32,1,128]{2,1,0:T(1,128)S(1)} %reshape.28), channel_id=1, replica_groups=mesh['slab'=32,'col'=4] {'slab'}, dimensions={0} | all-to-all | bytes 32768 | tf_op jit(solution)/shard_map/all_to_all | solution.py:122
  (44 shorter events, 34.1 us)
Async XLA Ops:
  0.6 8.6 %copy-start.5 = (f32[16,2,192,128]{3,2,1,0:T(8,128)S(1)}, f32[16,2,192,128]{3,2,1,0:T(8,128)}, u32[]{:S(2)}) copy-start(f32[16,2,192,128]{3,2,1,0:T(8,128)} %param.6) | copy-start | bytes 9437188
  14.3 4.6 copy-start.1
  14.3 11.4 %copy-start.7 = (f32[8]{0:T(128)S(1)}, f32[8]{0:T(128)}, u32[]{:S(2)}) copy-start(f32[8]{0:T(128)} %param.8) | copy-start | bytes 100
  14.4 12.1 %copy-start.6 = (s32[2,192,128]{2,1,0:T(8,128)S(1)}, s32[2,192,128]{2,1,0:T(8,128)}, u32[]{:S(2)}) copy-start(s32[2,192,128]{2,1,0:T(8,128)} %param.7) | copy-start | bytes 589828
  18.9 42.5 %collective-permute-start.1 = (f32[32,1,192,128]{3,2,1,0:T(8,128)}, f32[32,1,192,128]{3,2,1,0:T(8,128)}, u32[]{:S(2)}, u32[]{:S(2)}) collective-permute-start(f32[32,1,192,128]{3,2,1,0:T(8,128)} %get-tuple-element.22), channel_id=1, source_target_pairs={{4,0},{8,4},{12,8},{16,12},{20,16},{24,20},{28,24},{32,28},{36,32}... | collective-permute-start | bytes 9437192 | tf_op jit(solution)/shard_map/ppermute | solution.py:20
  22.3 39.2 %collective-permute-start.3 = (f32[32,1,192,128]{3,2,1,0:T(8,128)}, f32[32,1,192,128]{3,2,1,0:T(8,128)}, u32[]{:S(2)}, u32[]{:S(2)}) collective-permute-start(f32[32,1,192,128]{3,2,1,0:T(8,128)} %get-tuple-element.23), channel_id=1, source_target_pairs={{0,4},{4,8},{8,12},{12,16},{16,20},{20,24},{24,28},{28,32},{32,36}... | collective-permute-start | bytes 9437192 | tf_op jit(solution)/shard_map/ppermute | solution.py:17
  31.5 28.5 %collective-permute-start = (f32[1,192,128]{2,1,0:T(8,128)S(1)}, f32[1,192,128]{2,1,0:T(8,128)S(1)}, u32[]{:S(2)}, u32[]{:S(2)}) collective-permute-start(f32[1,192,128]{2,1,0:T(8,128)S(1)} %get-tuple-element.30), channel_id=1, source_target_pairs={{4,0},{8,4},{12,8},{16,12},{20,16},{24,20},{28,24},{32,28},{36,32}... | collective-permute-start | bytes 294920 | tf_op jit(solution)/shard_map/ppermute | solution.py:20
  34.0 27.2 %collective-permute-start.2 = (f32[1,192,128]{2,1,0:T(8,128)S(1)}, f32[1,192,128]{2,1,0:T(8,128)S(1)}, u32[]{:S(2)}, u32[]{:S(2)}) collective-permute-start(f32[1,192,128]{2,1,0:T(8,128)S(1)} %get-tuple-element.31), channel_id=1, source_target_pairs={{0,4},{4,8},{8,12},{12,16},{16,20},{20,24},{24,28},{28,32},{32,36}... | collective-permute-start | bytes 294920 | tf_op jit(solution)/shard_map/ppermute | solution.py:17
  84.8 4.6 copy-start.3
  89.4 39.6 %collective-permute-start.4 = (f32[32,1,192,128]{3,2,1,0:T(8,128)}, f32[32,1,192,128]{3,2,1,0:T(8,128)}, u32[]{:S(2)}, u32[]{:S(2)}) collective-permute-start(f32[32,1,192,128]{3,2,1,0:T(8,128)} %get-tuple-element.20), channel_id=1, source_target_pairs={{4,0},{8,4},{12,8},{16,12},{20,16},{24,20},{28,24},{32,28},{36,32}... | collective-permute-start | bytes 9437192 | tf_op jit(solution)/shard_map/ppermute | solution.py:20
  91.3 38.9 %collective-permute-start.5 = (f32[32,1,192,128]{3,2,1,0:T(8,128)}, f32[32,1,192,128]{3,2,1,0:T(8,128)}, u32[]{:S(2)}, u32[]{:S(2)}) collective-permute-start(f32[32,1,192,128]{3,2,1,0:T(8,128)} %get-tuple-element.21), channel_id=1, source_target_pairs={{0,4},{4,8},{8,12},{12,16},{16,20},{20,24},{24,28},{28,32},{32,36}... | collective-permute-start | bytes 9437192 | tf_op jit(solution)/shard_map/ppermute | solution.py:17
  156.1 4.6 copy-start.2
  160.7 39.6 %collective-permute-start.6 = (f32[32,1,192,128]{3,2,1,0:T(8,128)}, f32[32,1,192,128]{3,2,1,0:T(8,128)}, u32[]{:S(2)}, u32[]{:S(2)}) collective-permute-start(f32[32,1,192,128]{3,2,1,0:T(8,128)} %get-tuple-element.18), channel_id=1, source_target_pairs={{4,0},{8,4},{12,8},{16,12},{20,16},{24,20},{28,24},{32,28},{36,32}... | collective-permute-start | bytes 9437192 | tf_op jit(solution)/shard_map/ppermute | solution.py:20
  162.6 38.9 %collective-permute-start.7 = (f32[32,1,192,128]{3,2,1,0:T(8,128)}, f32[32,1,192,128]{3,2,1,0:T(8,128)}, u32[]{:S(2)}, u32[]{:S(2)}) collective-permute-start(f32[32,1,192,128]{3,2,1,0:T(8,128)} %get-tuple-element.19), channel_id=1, source_target_pairs={{0,4},{4,8},{8,12},{12,16},{16,20},{20,24},{24,28},{28,32},{32,36}... | collective-permute-start | bytes 9437192 | tf_op jit(solution)/shard_map/ppermute | solution.py:17
  228.1 4.6 copy-start
  232.7 39.6 %collective-permute-start.8 = (f32[32,1,192,128]{3,2,1,0:T(8,128)}, f32[32,1,192,128]{3,2,1,0:T(8,128)}, u32[]{:S(2)}, u32[]{:S(2)}) collective-permute-start(f32[32,1,192,128]{3,2,1,0:T(8,128)} %get-tuple-element.15), channel_id=1, source_target_pairs={{4,0},{8,4},{12,8},{16,12},{20,16},{24,20},{28,24},{32,28},{36,32}... | collective-permute-start | bytes 9437192 | tf_op jit(solution)/shard_map/ppermute | solution.py:20
  234.6 38.9 %collective-permute-start.9 = (f32[32,1,192,128]{3,2,1,0:T(8,128)}, f32[32,1,192,128]{3,2,1,0:T(8,128)}, u32[]{:S(2)}, u32[]{:S(2)}) collective-permute-start(f32[32,1,192,128]{3,2,1,0:T(8,128)} %get-tuple-element.16), channel_id=1, source_target_pairs={{0,4},{4,8},{8,12},{12,16},{16,20},{20,24},{24,28},{28,32},{32,36}... | collective-permute-start | bytes 9437192 | tf_op jit(solution)/shard_map/ppermute | solution.py:17
  273.5 27.1 %copy-start.4 = (f32[1,32,2,192,128]{4,3,2,1,0:T(8,128)S(1)}, f32[1,32,2,192,128]{4,3,2,1,0:T(8,128)}, u32[]{:S(2)}) copy-start(f32[1,32,2,192,128]{4,3,2,1,0:T(8,128)} %get-tuple-element.17) | copy-start | bytes 18874372
  311.2 66.6 %all-to-all-start.1 = ((f32[2,16,2,192,128]{4,2,1,0,3:T(2,128)}), f32[2,16,2,192,128]{4,2,1,0,3:T(2,128)}, u32[]{:S(2)}, u32[]{:S(2)}) async-start(f32[2,16,2,192,128]{4,2,1,0,3:T(2,128)} %copy.35), calls=%async_computation.1 | async-start | bytes 12582912 | tf_op jit(solution)/shard_map/all_to_all | solution.py:101
  377.8 47.3 %all-to-all-start = ((f32[2,16,2,192,128]{4,2,1,0,3:T(2,128)}), f32[2,16,2,192,128]{4,2,1,0,3:T(2,128)}, u32[]{:S(2)}, u32[]{:S(2)}) async-start(f32[2,16,2,192,128]{4,2,1,0,3:T(2,128)} %copy.33), calls=%async_computation | async-start | bytes 12582912 | tf_op jit(solution)/shard_map/all_to_all | solution.py:100

commit v3 on v2

--- a/solution.py
+++ b/solution.py
@@ -3,6 +3,8 @@
 import jax
 import jax.numpy as jnp
 from jax import lax
+from jax.experimental import pallas as pl
+from jax.experimental.pallas import tpu as pltpu
 from jax.sharding import PartitionSpec as P
 
 ADI = 2
@@ -20,6 +22,71 @@
         high = lax.ppermute(lax.slice_in_dim(block, 0, width, axis=dim), axis, backward)
         block = jnp.concatenate([low, block, high], axis=dim)
     return block
+
+
+def scatter_sum_kernel(tiles_ref, out_ref, recv, send_sem, recv_sem):
+    count = tiles_ref.shape[0]
+    me = lax.axis_index("slab")
+    col = lax.axis_index("col")
+    recv[pl.ds(me, 1)] = tiles_ref[pl.ds(me, 1)]
+    barrier = pltpu.get_barrier_semaphore()
+
+    def greet(k, carry):
+        peer = lax.rem(me + k, count)
+        pl.semaphore_signal(barrier, inc=1, device_id=(peer, col), device_id_type=pl.DeviceIdType.MESH)
+        return carry
+
+    lax.fori_loop(1, count, greet, 0)
+    pl.semaphore_wait(barrier, count - 1)
+
+    def copy_to(k):
+        peer = lax.rem(me + k, count)
+        return pltpu.make_async_remote_copy(
+            src_ref=tiles_ref.at[pl.ds(peer, 1)],
+            dst_ref=recv.at[pl.ds(me, 1)],
+            send_sem=send_sem.at[peer],
+            recv_sem=recv_sem.at[me],
+            device_id=(peer, col),
+            device_id_type=pl.DeviceIdType.MESH,
+        )
+
+    def send(k, carry):
+        copy_to(k).start()
+        return carry
+
+    lax.fori_loop(1, count, send, 0)
+
+    def finish(k, carry):
+        peer = lax.rem(me + k, count)
+        copy_to(k).wait_send()
+        pltpu.make_async_remote_copy(
+            src_ref=tiles_ref.at[pl.ds(me, 1)],
+            dst_ref=recv.at[pl.ds(peer, 1)],
+            send_sem=send_sem.at[me],
+            recv_sem=recv_sem.at[peer],
+            device_id=(peer, col),
+            device_id_type=pl.DeviceIdType.MESH,
+        ).wait_recv()
+        return carry
+
+    lax.fori_loop(1, count, finish, 0)
+    out_ref[...] = jnp.sum(recv[...], axis=0, keepdims=True)
+
+
+def scatter_sum(tiles):
+    count, rows, lanes = tiles.shape
+    return pl.pallas_call(
+        scatter_sum_kernel,
+        out_shape=jax.ShapeDtypeStruct((1, rows, lanes), jnp.float32),
+        in_specs=[pl.BlockSpec(memory_space=pltpu.VMEM)],
+        out_specs=pl.BlockSpec(memory_space=pltpu.VMEM),
+        scratch_shapes=[
+            pltpu.VMEM((count, rows, lanes), jnp.float32),
+            pltpu.SemaphoreType.DMA((count,)),
+            pltpu.SemaphoreType.DMA((count,)),
+        ],
+        compiler_params=pltpu.CompilerParams(collective_id=0, has_side_effects=True),
+    )(tiles)
 
 
 def lookup(region_ids, region_cond):
@@ -118,8 +185,8 @@
     tile_cols = row_count // col_count
     col_parts = partial_value.reshape(row_count, col_count, tile_cols).transpose(1, 0, 2)
     col_sum = jnp.sum(lax.all_to_all(col_parts, "col", 0, 0, tiled=True), axis=0)
-    row_parts = col_sum.reshape(slab_count, tile_rows, tile_cols)
-    own_tile = jnp.sum(lax.all_to_all(row_parts, "slab", 0, 0, tiled=True), axis=0)
+    row_parts = col_sum.reshape(slab_count, 1, tile_rows * tile_cols)
+    own_tile = scatter_sum(row_parts).reshape(tile_rows, tile_cols)
     return (ctrl_cols, obsv_cols, own_tile * norm_scale)
 
 

time: 517 us -> 515 us (level)
  blocking collectives: 63.4 us -> 6.84 us
  Pallas kernels: 0 us -> 55.2 us
    all_to_all x1 -> x0, blocking collectives: 56.5 us -> none  [body(): lax.all_to_all(row_parts, 'slab', 0, 0, tiled=True)]
    pallas_call x0 -> x1, Pallas kernels: none -> 55.2 us  [scatter_sum(): pl.pallas_call(scatter_sum_kernel, out_shape=jax.ShapeDtypeStruct((1, row...]
where the time goes in v3:
time: 515 us; the launch traced here: 514 us
  waiting for transfers between devices  198 us (38%)
  other arithmetic  117 us (23%)
  local copies, waits for them, and re-layouts  77.8 us (15%)
  Pallas kernels  55.2 us (11%)
  starting transfers between devices  42.2 us (8%)
  between operations  8.79 us (2%)
  matrix products  8.21 us (2%)
  blocking collectives  6.84 us (1%)
    ppermute x5, waiting for transfers between devices, extended(): lax.ppermute(lax.slice_in_dim(block, 0, width, axis=dim), axis, backward)  117 us
    pallas_call x1, Pallas kernels, scatter_sum(): pl.pallas_call(scatter_sum_kernel, out_shape=jax.ShapeDtypeStruct((1, row...  55.2 us
    all_to_all x1, waiting for transfers between devices, body(): lax.all_to_all(obsv_local, 'col', split_axis=3, concat_axis=1, tiled=True)  50.9 us
    add x2, other arithmetic, solve_slabs(): rho_next * rho_now * direction + 2.0 * rho_next / half_span * residual  49.9 us
    another operation x2, other arithmetic, run_segments(): return jnp.stack(factors)  30.2 us
    div x2, other arithmetic, solve_slabs(): direction = right_side / mid_eig  29.1 us
    all_to_all x1, waiting for transfers between devices, body(): lax.all_to_all(ctrl_local, 'col', split_axis=3, concat_axis=1, tiled=True)  25.3 us
    ppermute x5, starting transfers between devices, extended(): lax.ppermute(lax.slice_in_dim(block, block.shape[dim] - width, None, axis...  19.9 us
  transfers between devices with their start and end apart: 12, of which 10 were waited for; matrix products, arithmetic and copies ran while one was open for 6% of the time, Pallas kernels for 0%

profile of v3, /device:TPU:1, one launch (start us, length us, event | category | flops | bytes accessed | tf_op | source)
XLA Modules:
  0.0 514.0 jit_solution(10919526858251335570)
XLA Ops:
  5.3 3.9 constant_dynamic-update-slice_fusion.1
  14.4 3.3 fusion.105
  18.9 3.3 collective-permute-start.1
  22.3 3.5 collective-permute-start.3
  26.5 4.9 select_add_fusion
  37.8 22.2 %collective-permute-done = f32[1,192,128]{2,1,0:T(8,128)S(1)} collective-permute-done((f32[1,192,128]{2,1,0:T(8,128)S(1)}, f32[1,192,128]{2,1,0:T(8,128)S(1)}, u32[]{:S(2)}, u32[]{:S(2)}) %collective-permute-start) | collective-permute-done | bytes 98336 | tf_op jit(solution)/shard_map/ppermute | solution.py:22
  61.5 23.3 %multiply_add_fusion.1 = (f32[32,2,192,128]{3,2,1,0:T(8,128)S(1)}, f32[32,2,192,128]{3,2,1,0:T(8,128)}) fusion(f32[32,2,192,128]{3,2,1,0:T(8,128)} %copy-done.1, f32[]{:T(128)S(6)} %div.53, f32[]{:T(128)S(6)} %mul.351, f32[32,2,192,128]{3,2,1,0:T(8,128)} %constant_dynamic-update-slice_fusion, f32[]{:T(128)} %bitcast, ...), kind=kLoop, calls=%fused_computation.116 | loop fusion | flops 39321600 | bytes 32636940 | tf_op jit(solution)/shard_map/add | solution.py:134
  84.8 3.3 fusion.104
  91.3 4.4 collective-permute-start.5
  97.2 31.9 %collective-permute-done.4 = f32[32,1,192,128]{3,2,1,0:T(8,128)} collective-permute-done((f32[32,1,192,128]{3,2,1,0:T(8,128)}, f32[32,1,192,128]{3,2,1,0:T(8,128)}, u32[]{:S(2)}, u32[]{:S(2)}) %collective-permute-start.4) | collective-permute-done | bytes 3145760 | tf_op jit(solution)/shard_map/ppermute | solution.py:22
  130.2 25.9 %broadcast_divide_fusion = (f32[32,2,192,128]{3,2,1,0:T(8,128)S(1)}, f32[32,2,192,128]{3,2,1,0:T(8,128)}) fusion(f32[]{:T(128)S(6)} %mul.394, f32[32,2,192,128]{3,2,1,0:T(8,128)} %get-tuple-element.8, f32[32,2,192,128]{3,2,1,0:T(8,128)} %copy-done.3, f32[]{:T(128)} %bitcast, f32[2,192,128]{2,1,0:T(8,128)S(1)} %get-tuple-element.29, ...), kind=kLoop, calls=%fused_computation.117 | loop fusion | flops 45613056 | bytes 38928404 | tf_op jit(solution)/shard_map/div | solution.py:127
  156.1 3.8 fusion.103
  162.6 4.4 collective-permute-start.7
  168.5 31.8 %collective-permute-done.6 = f32[32,1,192,128]{3,2,1,0:T(8,128)} collective-permute-done((f32[32,1,192,128]{3,2,1,0:T(8,128)}, f32[32,1,192,128]{3,2,1,0:T(8,128)}, u32[]{:S(2)}, u32[]{:S(2)}) %collective-permute-start.6) | collective-permute-done | bytes 3145760 | tf_op jit(solution)/shard_map/ppermute | solution.py:22
  201.5 26.6 %multiply_add_fusion = (f32[32,2,192,128]{3,2,1,0:T(8,128)S(1)}, f32[32,2,192,128]{3,2,1,0:T(8,128)}, f32[1,32,2,192,128]{4,3,2,1,0:T(8,128)}) fusion(f32[]{:T(128)S(6)} %div.61, f32[]{:T(128)S(6)} %mul.397, f32[32,2,192,128]{3,2,1,0:T(8,128)} %get-tuple-element.6, f32[]{:T(128)S(6)} %mul.394, f32[32,2,192,128]{3,2,1,0:T(8,128)} %copy-done.2, f32[]{:T(128)} %bitcast.10, ...), kind=kLoop, calls=%fused_computation.114 | loop fusion | flops 42467328 | bytes 38928404 | tf_op jit(solution)/shard_map/add | solution.py:134
  228.1 3.8 fusion.102
  234.6 4.6 collective-permute-start.9
  241.4 31.0 %collective-permute-done.8 = f32[32,1,192,128]{3,2,1,0:T(8,128)} collective-permute-done((f32[32,1,192,128]{3,2,1,0:T(8,128)}, f32[32,1,192,128]{3,2,1,0:T(8,128)}, u32[]{:S(2)}, u32[]{:S(2)}) %collective-permute-start.8) | collective-permute-done | bytes 3145760 | tf_op jit(solution)/shard_map/ppermute | solution.py:22
  273.5 27.1 %fusion.47 = f32[1,32,2,192,128]{4,3,2,1,0:T(8,128)S(1)} fusion(f32[32,2,192,128]{3,2,1,0:T(8,128)} %get-tuple-element.6, f32[32,2,192,128]{3,2,1,0:T(8,128)} %get-tuple-element.4, f32[32,2,192,128]{3,2,1,0:T(8,128)} %copy-done, f32[32,1,192,128]{3,2,1,0:T(8,128)} %collective-permute-done.9, f32[32,1,192,128]{3,2,1,0:T(8,128)} %collective-permute-done.8, ...), kind=kLoop, calls=%fused_computation.65 | loop fusion | flops 48758784 | bytes 32636952 | tf_op jit(solution)/shard_map/stack | solution.py:149
  303.8 7.5 %copy.28 = f32[2,16,2,192,128]{4,2,1,0,3:T(2,128)} copy(f32[2,16,2,192,128]{4,3,2,1,0:T(8,128)S(1)} %get-tuple-element.9) | data formatting | bytes 12582912 | tf_op jit(solution)/shard_map/slice | solution.py:165
  311.3 5.2 %all-to-all-start.1 = ((f32[2,16,2,192,128]{4,2,1,0,3:T(2,128)}), f32[2,16,2,192,128]{4,2,1,0,3:T(2,128)}, u32[]{:S(2)}, u32[]{:S(2)}) async-start(f32[2,16,2,192,128]{4,2,1,0,3:T(2,128)} %copy.28), calls=%async_computation.1 | async-start | bytes 12582912 | tf_op jit(solution)/shard_map/all_to_all | solution.py:168
  316.5 10.3 %copy.26 = f32[2,16,2,192,128]{4,2,1,0,3:T(2,128)} copy(f32[2,16,2,192,128]{4,3,2,1,0:T(8,128)} %get-tuple-element.10) | data formatting | bytes 12582912 | tf_op jit(solution)/shard_map/slice | solution.py:164
  326.9 50.9 %all-to-all-done.1 = f32[2,16,2,192,128]{4,2,1,0,3:T(2,128)} async-done(((f32[2,16,2,192,128]{4,2,1,0,3:T(2,128)}), f32[2,16,2,192,128]{4,2,1,0,3:T(2,128)}, u32[]{:S(2)}, u32[]{:S(2)}) %all-to-all-start.1) | async-done | bytes 6291488 | tf_op jit(solution)/shard_map/all_to_all | solution.py:168
  377.8 5.5 %all-to-all-start = ((f32[2,16,2,192,128]{4,2,1,0,3:T(2,128)}), f32[2,16,2,192,128]{4,2,1,0,3:T(2,128)}, u32[]{:S(2)}, u32[]{:S(2)}) async-start(f32[2,16,2,192,128]{4,2,1,0,3:T(2,128)} %copy.26), calls=%async_computation | async-start | bytes 12582912 | tf_op jit(solution)/shard_map/all_to_all | solution.py:167
  383.3 9.0 %copy.36 = f32[2,16,2,4,48,128]{5,4,2,1,3,0:T(8,128)} copy(f32[2,16,2,4,48,128]{5,2,1,0,4,3:T(2,128)} %bitcast.15) | data formatting | bytes 12582912 | tf_op jit(solution)/shard_map/all_to_all | solution.py:168
  392.4 7.4 %dot_general.5 = f32[4,32,12288]{2,1,0:T(8,128)} reshape(f32[2,4,16,2,48,128]{5,4,3,2,1,0:T(8,128)} %bitcast.35) | data formatting | bytes 12582912 | tf_op jit(solution)/shard_map/dot_general | solution.py:173
  399.8 25.3 %all-to-all-done = f32[2,16,2,192,128]{4,2,1,0,3:T(2,128)} async-done(((f32[2,16,2,192,128]{4,2,1,0,3:T(2,128)}), f32[2,16,2,192,128]{4,2,1,0,3:T(2,128)}, u32[]{:S(2)}, u32[]{:S(2)}) %all-to-all-start) | async-done | bytes 6291488 | tf_op jit(solution)/shard_map/all_to_all | solution.py:167
  425.1 9.0 %copy.37 = f32[2,16,2,4,48,128]{5,4,2,1,3,0:T(8,128)} copy(f32[2,16,2,4,48,128]{5,2,1,0,4,3:T(2,128)} %bitcast.12) | data formatting | bytes 12582912 | tf_op jit(solution)/shard_map/all_to_all | solution.py:167
  434.2 7.5 %reshape.29 = f32[128,12288,1]{1,0,2:T(8,128)} reshape(f32[2,4,16,2,48,128]{5,4,3,2,1,0:T(8,128)} %bitcast.37) | data formatting | bytes 12582912 | tf_op jit(solution)/shard_map/reshape | solution.py:171
  441.6 8.2 %convolution_bitcast_fusion = f32[4,128,32]{1,2,0:T(8,128)S(1)} fusion(f32[128,12288,1]{1,0,2:T(8,128)} %reshape.29, f32[4,32,12288]{2,1,0:T(8,128)} %dot_general.5), kind=kOutput, calls=%fused_computation.119 | convolution fusion | flops 2415919104 | bytes 12648448 | tf_op jit(solution)/shard_map/dot_general | solution.py:173
  449.9 6.8 %all_to_all.41 = f32[4,128,32]{1,2,0:T(8,128)S(1)} all-to-all(f32[4,128,32]{1,2,0:T(8,128)S(1)} %convolution_bitcast_fusion), channel_id=1, replica_groups=mesh['slab'=32,'col'=4] {'col'}, dimensions={0} | all-to-all | bytes 131072 | tf_op jit(solution)/shard_map/all_to_all | solution.py:187
  457.5 55.2 %shard_map.76 = f32[1,1,128]{2,1,0:T(1,128)} custom-call(f32[32,1,128]{2,1,0:T(1,128)} %bitcast.39), custom_call_target="tpu_custom_call" | custom-call | tf_op jit(solution)/shard_map/pallas_call | solution.py:78
  (41 shorter events, 34.1 us)
Async XLA Ops:
  0.6 8.6 %copy-start.5 = (f32[16,2,192,128]{3,2,1,0:T(8,128)S(1)}, f32[16,2,192,128]{3,2,1,0:T(8,128)}, u32[]{:S(2)}) copy-start(f32[16,2,192,128]{3,2,1,0:T(8,128)} %param.6) | copy-start | bytes 9437188
  14.3 4.6 copy-start.1
  14.4 11.4 %copy-start.7 = (f32[8]{0:T(128)S(1)}, f32[8]{0:T(128)}, u32[]{:S(2)}) copy-start(f32[8]{0:T(128)} %param.8) | copy-start | bytes 100
  14.4 12.1 %copy-start.6 = (s32[2,192,128]{2,1,0:T(8,128)S(1)}, s32[2,192,128]{2,1,0:T(8,128)}, u32[]{:S(2)}) copy-start(s32[2,192,128]{2,1,0:T(8,128)} %param.7) | copy-start | bytes 589828
  18.9 42.5 %collective-permute-start.1 = (f32[32,1,192,128]{3,2,1,0:T(8,128)}, f32[32,1,192,128]{3,2,1,0:T(8,128)}, u32[]{:S(2)}, u32[]{:S(2)}) collective-permute-start(f32[32,1,192,128]{3,2,1,0:T(8,128)} %get-tuple-element.22), channel_id=1, source_target_pairs={{4,0},{8,4},{12,8},{16,12},{20,16},{24,20},{28,24},{32,28},{36,32}... | collective-permute-start | bytes 9437192 | tf_op jit(solution)/shard_map/ppermute | solution.py:22
  22.3 39.2 %collective-permute-start.3 = (f32[32,1,192,128]{3,2,1,0:T(8,128)}, f32[32,1,192,128]{3,2,1,0:T(8,128)}, u32[]{:S(2)}, u32[]{:S(2)}) collective-permute-start(f32[32,1,192,128]{3,2,1,0:T(8,128)} %get-tuple-element.23), channel_id=1, source_target_pairs={{0,4},{4,8},{8,12},{12,16},{16,20},{20,24},{24,28},{28,32},{32,36}... | collective-permute-start | bytes 9437192 | tf_op jit(solution)/shard_map/ppermute | solution.py:19
  31.4 28.6 %collective-permute-start = (f32[1,192,128]{2,1,0:T(8,128)S(1)}, f32[1,192,128]{2,1,0:T(8,128)S(1)}, u32[]{:S(2)}, u32[]{:S(2)}) collective-permute-start(f32[1,192,128]{2,1,0:T(8,128)S(1)} %get-tuple-element.30), channel_id=1, source_target_pairs={{4,0},{8,4},{12,8},{16,12},{20,16},{24,20},{28,24},{32,28},{36,32}... | collective-permute-start | bytes 294920 | tf_op jit(solution)/shard_map/ppermute | solution.py:22
  34.0 27.3 %collective-permute-start.2 = (f32[1,192,128]{2,1,0:T(8,128)S(1)}, f32[1,192,128]{2,1,0:T(8,128)S(1)}, u32[]{:S(2)}, u32[]{:S(2)}) collective-permute-start(f32[1,192,128]{2,1,0:T(8,128)S(1)} %get-tuple-element.31), channel_id=1, source_target_pairs={{0,4},{4,8},{8,12},{12,16},{16,20},{20,24},{24,28},{28,32},{32,36}... | collective-permute-start | bytes 294920 | tf_op jit(solution)/shard_map/ppermute | solution.py:19
  84.8 4.6 copy-start.3
  89.4 39.6 %collective-permute-start.4 = (f32[32,1,192,128]{3,2,1,0:T(8,128)}, f32[32,1,192,128]{3,2,1,0:T(8,128)}, u32[]{:S(2)}, u32[]{:S(2)}) collective-permute-start(f32[32,1,192,128]{3,2,1,0:T(8,128)} %get-tuple-element.20), channel_id=1, source_target_pairs={{4,0},{8,4},{12,8},{16,12},{20,16},{24,20},{28,24},{32,28},{36,32}... | collective-permute-start | bytes 9437192 | tf_op jit(solution)/shard_map/ppermute | solution.py:22
  91.3 38.9 %collective-permute-start.5 = (f32[32,1,192,128]{3,2,1,0:T(8,128)}, f32[32,1,192,128]{3,2,1,0:T(8,128)}, u32[]{:S(2)}, u32[]{:S(2)}) collective-permute-start(f32[32,1,192,128]{3,2,1,0:T(8,128)} %get-tuple-element.21), channel_id=1, source_target_pairs={{0,4},{4,8},{8,12},{12,16},{16,20},{20,24},{24,28},{28,32},{32,36}... | collective-permute-start | bytes 9437192 | tf_op jit(solution)/shard_map/ppermute | solution.py:19
  156.1 4.6 copy-start.2
  160.7 39.6 %collective-permute-start.6 = (f32[32,1,192,128]{3,2,1,0:T(8,128)}, f32[32,1,192,128]{3,2,1,0:T(8,128)}, u32[]{:S(2)}, u32[]{:S(2)}) collective-permute-start(f32[32,1,192,128]{3,2,1,0:T(8,128)} %get-tuple-element.18), channel_id=1, source_target_pairs={{4,0},{8,4},{12,8},{16,12},{20,16},{24,20},{28,24},{32,28},{36,32}... | collective-permute-start | bytes 9437192 | tf_op jit(solution)/shard_map/ppermute | solution.py:22
  162.6 38.9 %collective-permute-start.7 = (f32[32,1,192,128]{3,2,1,0:T(8,128)}, f32[32,1,192,128]{3,2,1,0:T(8,128)}, u32[]{:S(2)}, u32[]{:S(2)}) collective-permute-start(f32[32,1,192,128]{3,2,1,0:T(8,128)} %get-tuple-element.19), channel_id=1, source_target_pairs={{0,4},{4,8},{8,12},{12,16},{16,20},{20,24},{24,28},{28,32},{32,36}... | collective-permute-start | bytes 9437192 | tf_op jit(solution)/shard_map/ppermute | solution.py:19
  228.1 4.6 copy-start
  232.7 39.6 %collective-permute-start.8 = (f32[32,1,192,128]{3,2,1,0:T(8,128)}, f32[32,1,192,128]{3,2,1,0:T(8,128)}, u32[]{:S(2)}, u32[]{:S(2)}) collective-permute-start(f32[32,1,192,128]{3,2,1,0:T(8,128)} %get-tuple-element.15), channel_id=1, source_target_pairs={{4,0},{8,4},{12,8},{16,12},{20,16},{24,20},{28,24},{32,28},{36,32}... | collective-permute-start | bytes 9437192 | tf_op jit(solution)/shard_map/ppermute | solution.py:22
  234.6 38.9 %collective-permute-start.9 = (f32[32,1,192,128]{3,2,1,0:T(8,128)}, f32[32,1,192,128]{3,2,1,0:T(8,128)}, u32[]{:S(2)}, u32[]{:S(2)}) collective-permute-start(f32[32,1,192,128]{3,2,1,0:T(8,128)} %get-tuple-element.16), channel_id=1, source_target_pairs={{0,4},{4,8},{8,12},{12,16},{16,20},{20,24},{24,28},{28,32},{32,36}... | collective-permute-start | bytes 9437192 | tf_op jit(solution)/shard_map/ppermute | solution.py:19
  273.5 27.1 %copy-start.4 = (f32[1,32,2,192,128]{4,3,2,1,0:T(8,128)S(1)}, f32[1,32,2,192,128]{4,3,2,1,0:T(8,128)}, u32[]{:S(2)}) copy-start(f32[1,32,2,192,128]{4,3,2,1,0:T(8,128)} %get-tuple-element.17) | copy-start | bytes 18874372
  311.3 66.5 %all-to-all-start.1 = ((f32[2,16,2,192,128]{4,2,1,0,3:T(2,128)}), f32[2,16,2,192,128]{4,2,1,0,3:T(2,128)}, u32[]{:S(2)}, u32[]{:S(2)}) async-start(f32[2,16,2,192,128]{4,2,1,0,3:T(2,128)} %copy.28), calls=%async_computation.1 | async-start | bytes 12582912 | tf_op jit(solution)/shard_map/all_to_all | solution.py:168
  377.8 47.3 %all-to-all-start = ((f32[2,16,2,192,128]{4,2,1,0,3:T(2,128)}), f32[2,16,2,192,128]{4,2,1,0,3:T(2,128)}, u32[]{:S(2)}, u32[]{:S(2)}) async-start(f32[2,16,2,192,128]{4,2,1,0,3:T(2,128)} %copy.26), calls=%async_computation | async-start | bytes 12582912 | tf_op jit(solution)/shard_map/all_to_all | solution.py:167

commit v4 on v3

--- a/solution.py
+++ b/solution.py
@@ -96,19 +96,48 @@
     return summed
 
 
-def conduction(field_in, cond_ext):
-    centre = field_in[:, 1:-1]
-    cond_mid = cond_ext[1:-1]
-    summed = 0.5 * (cond_mid + cond_ext[2:]) * (centre - field_in[:, 2:])
-    summed = summed + 0.5 * (cond_mid + cond_ext[:-2]) * (centre - field_in[:, :-2])
-    cond_y = jnp.pad(cond_mid, ((0, 0), (1, 1), (0, 0)))
-    field_y = jnp.pad(centre, ((0, 0), (0, 0), (1, 1), (0, 0)))
-    summed = summed + 0.5 * (cond_mid + cond_y[:, 2:]) * (centre - field_y[:, :, 2:])
-    summed = summed + 0.5 * (cond_mid + cond_y[:, :-2]) * (centre - field_y[:, :, :-2])
+def halo_pair(block, axis, dim):
+    count = lax.axis_size(axis)
+    forward = [(i, i + 1) for i in range(count - 1)]
+    backward = [(target, source) for source, target in forward]
+    size = block.shape[dim]
+    low = lax.ppermute(lax.slice_in_dim(block, size - 1, None, axis=dim), axis, forward)
+    high = lax.ppermute(lax.slice_in_dim(block, 0, 1, axis=dim), axis, backward)
+    return low, high
+
+
+def shifted(block, low, high, dim):
+    size = block.shape[dim]
+    ahead = jnp.concatenate([lax.slice_in_dim(block, 1, None, axis=dim), high], axis=dim)
+    behind = jnp.concatenate([low, lax.slice_in_dim(block, 0, size - 1, axis=dim)], axis=dim)
+    return ahead, behind
+
+
+def coefficients(cond_xy):
+    cond_mid = cond_xy[1:-1, 1:-1]
+    kxp = 0.5 * (cond_mid + cond_xy[2:, 1:-1])
+    kxm = 0.5 * (cond_mid + cond_xy[:-2, 1:-1])
+    kyp = 0.5 * (cond_mid + cond_xy[1:-1, 2:])
+    kym = 0.5 * (cond_mid + cond_xy[1:-1, :-2])
     cond_z = jnp.pad(cond_mid, ((0, 0), (0, 0), (1, 1)))
-    field_z = jnp.pad(centre, ((0, 0), (0, 0), (0, 0), (1, 1)))
-    summed = summed + 0.5 * (cond_mid + cond_z[:, :, 2:]) * (centre - field_z[:, :, :, 2:])
-    summed = summed + 0.5 * (cond_mid + cond_z[:, :, :-2]) * (centre - field_z[:, :, :, :-2])
+    kzp = 0.5 * (cond_mid + cond_z[:, :, 2:])
+    kzm = 0.5 * (cond_mid + cond_z[:, :, :-2])
+    return (kxp, kxm, kyp, kym, kzp, kzm)
+
+
+def conduction(field, coeffs):
+    kxp, kxm, kyp, kym, kzp, kzm = coeffs
+    xlo, xhi = halo_pair(field, "slab", 1)
+    ylo, yhi = halo_pair(field, "col", 2)
+    nxp, nxm = shifted(field, xlo, xhi, 1)
+    nyp, nym = shifted(field, ylo, yhi, 2)
+    field_z = jnp.pad(field, ((0, 0), (0, 0), (0, 0), (1, 1)))
+    summed = kxp * (field - nxp)
+    summed = summed + kxm * (field - nxm)
+    summed = summed + kyp * (field - nyp)
+    summed = summed + kym * (field - nym)
+    summed = summed + kzp * (field - field_z[..., 2:])
+    summed = summed + kzm * (field - field_z[..., :-2])
     return summed
 
 
@@ -119,7 +148,7 @@
     return (mid_eig, half_span, mid_eig / half_span)
 
 
-def solve_slabs(right_side, shift_val, cond_max, cond_ext):
+def solve_slabs(right_side, shift_val, cond_max, coeffs):
     mid_eig, half_span, ratio_eig = bounds(shift_val, cond_max)
     rho_now = 1.0 / ratio_eig
     solution = jnp.zeros_like(right_side)
@@ -127,8 +156,7 @@
     direction = right_side / mid_eig
     for sweep_idx in range(STEPS - 1):
         solution = solution + direction
-        padded = extended(direction, (("slab", 1),), 1)
-        applied = conduction(padded, cond_ext) + shift_val * direction
+        applied = conduction(direction, coeffs) + shift_val * direction
         residual = residual - applied
         rho_next = 1.0 / (2.0 * ratio_eig - rho_now)
         direction = rho_next * rho_now * direction + 2.0 * rho_next / half_span * residual
@@ -150,23 +178,25 @@
 
 
 def body(input_map, output_map, region_ids, region_cond, shift_ids):
-    col_local = input_map.shape[0]
+    ctrl_in = lax.all_to_all(input_map, "col", 2, 0, tiled=True)
+    obsv_in = lax.all_to_all(output_map, "col", 2, 0, tiled=True)
+    col_local = ctrl_in.shape[0]
+    rows = ctrl_in.shape[2]
     local_x = input_map.shape[1]
     cond_cells = lookup(region_ids, region_cond)
     cond_max = jnp.max(region_cond)
     shifts = 0.25 * jnp.exp2(shift_ids.astype(jnp.float32))
     total_x = local_x * lax.axis_size("slab")
-    stacked = jnp.concatenate([input_map, output_map], 0)
-    cond_ext = extended(cond_cells, (("slab", 0),), 1)
+    stacked = jnp.concatenate([ctrl_in, obsv_in], 0)
+    cond_ypad = jnp.pad(cond_cells, ((0, 0), (1, 1), (0, 0)))
+    cond_y = lax.dynamic_slice_in_dim(cond_ypad, lax.axis_index("col") * rows, rows + 2, axis=1)
+    cond_xy = extended(cond_y, (("slab", 0),), 1)
+    coeffs = coefficients(cond_xy)
     factor_stack = run_segments(
-        stacked, shifts, lambda rhs, shift_val: solve_slabs(rhs, shift_val, cond_max, cond_ext)
-    )
-    ctrl_local = factor_stack[:, :col_local]
-    obsv_local = factor_stack[:, col_local:]
-    ctrl_cols, obsv_cols = (
-        lax.all_to_all(ctrl_local, "col", split_axis=3, concat_axis=1, tiled=True),
-        lax.all_to_all(obsv_local, "col", split_axis=3, concat_axis=1, tiled=True),
-    )
+        stacked, shifts, lambda rhs, shift_val: solve_slabs(rhs, shift_val, cond_max, coeffs)
+    )
+    ctrl_cols = factor_stack[:, :col_local]
+    obsv_cols = factor_stack[:, col_local:]
     row_count = ctrl_cols.shape[0] * ctrl_cols.shape[1]
     ctrl_flat = ctrl_cols.reshape(row_count, -1)
     obsv_flat = obsv_cols.reshape(row_count, -1)

time: 515 us -> 434 us (0.84)
  waiting for transfers between devices: 198 us -> 121 us
  Pallas kernels: 55.2 us -> 22 us
  local copies, waits for them, and re-layouts: 77.8 us -> 105 us
  starting transfers between devices: 42.2 us -> 67.2 us
  other arithmetic: 117 us -> 92.6 us
    ppermute x5 -> x1, waiting for transfers between devices: 117 us -> 21 us  [extended(): lax.ppermute(lax.slice_in_dim(block, 0, width, axis=dim), axis, backward)]
    ppermute x0 -> x16, starting transfers between devices: none -> 52.1 us  [the longest x8 36.5 us: halo_pair(): lax.ppermute(lax.slice_in_dim(block, size - 1, None, axis=dim), axis, for...]
    ppermute x0 -> x16, waiting for transfers between devices: none -> 39 us  [the longest x8 35.5 us: halo_pair(): high = lax.ppermute(lax.slice_in_dim(block, 0, 1, axis=dim), axis, backward)]
    pallas_call x1, Pallas kernels: 55.2 us -> 22 us  [scatter_sum(): pl.pallas_call(scatter_sum_kernel, out_shape=jax.ShapeDtypeStruct((1, row...]
    slice x7 -> x13, local copies, waits for them, and re-layouts: 32 us -> 64.6 us  [the longest x7 50.1 us: shifted(): lax.slice_in_dim(block, 1, None, axis=dim)]
    ppermute x5 -> x1, starting transfers between devices: 19.9 us -> 3.03 us  [extended(): lax.ppermute(lax.slice_in_dim(block, block.shape[dim] - width, None, axis...]
    all_to_all x2, waiting for transfers between devices: 76.3 us -> 60.1 us  [the longest x1 31.2 us: body(): ctrl_in = lax.all_to_all(input_map, 'col', 2, 0, tiled=True)]
    add x2, other arithmetic: 49.9 us -> 35.4 us  [solve_slabs(): rho_next * rho_now * direction + 2.0 * rho_next / half_span * residual]
  transfers between devices with their start and end apart: 12 -> 20, of which waited for: 10 -> 10; matrix products, arithmetic and copies ran while one was open for 6% -> 16% of each run, Pallas kernels for 0% -> 0%
where the time goes in v4:
time: 434 us; the launch traced here: 432 us
  waiting for transfers between devices  121 us (28%)
  local copies, waits for them, and re-layouts  105 us (24%)
  other arithmetic  92.6 us (21%)
  starting transfers between devices  67.2 us (15%)
  Pallas kernels  22 us (5%)
  between operations  8.94 us (2%)
  matrix products  8.21 us (2%)
  blocking collectives  6.84 us (2%)
    slice x7, local copies, waits for them, and re-layouts, shifted(): lax.slice_in_dim(block, 1, None, axis=dim)  50.1 us
    ppermute x8, starting transfers between devices, halo_pair(): lax.ppermute(lax.slice_in_dim(block, size - 1, None, axis=dim), axis, for...  36.5 us
    ppermute x8, waiting for transfers between devices, halo_pair(): high = lax.ppermute(lax.slice_in_dim(block, 0, 1, axis=dim), axis, backward)  35.5 us
    add x2, other arithmetic, solve_slabs(): rho_next * rho_now * direction + 2.0 * rho_next / half_span * residual  35.4 us
    all_to_all x1, waiting for transfers between devices, body(): ctrl_in = lax.all_to_all(input_map, 'col', 2, 0, tiled=True)  31.2 us
    all_to_all x1, waiting for transfers between devices, body(): obsv_in = lax.all_to_all(output_map, 'col', 2, 0, tiled=True)  28.8 us
    another operation x3, other arithmetic, run_segments(): return jnp.stack(factors)  26.6 us
    div x2, other arithmetic, solve_slabs(): direction = right_side / mid_eig  23.8 us
  transfers between devices with their start and end apart: 20, of which 10 were waited for; matrix products, arithmetic and copies ran while one was open for 16% of the time, Pallas kernels for 0%

profile of v4, /device:TPU:1, one launch (start us, length us, event | category | flops | bytes accessed | tf_op | source)
XLA Modules:
  0.0 432.0 jit_solution(261081231511324510)
XLA Ops:
  0.6 5.4 %copy.19 = f32[16,2,192,128]{3,0,1,2:T(8,128)} copy(f32[16,2,192,128]{3,2,1,0:T(8,128)} %param.5) | data formatting | bytes 6291456 | tf_op args[0]
  6.0 4.8 %all-to-all-start = ((f32[16,2,192,128]{3,0,1,2:T(8,128)}), f32[16,2,192,128]{3,0,1,2:T(8,128)S(1)}, u32[]{:S(2)}, u32[]{:S(2)}) async-start(f32[16,2,192,128]{3,0,1,2:T(8,128)} %copy.19), calls=%async_computation | async-start | bytes 6291456 | tf_op jit(solution)/shard_map/all_to_all | solution.py:181
  10.9 5.4 %copy.21 = f32[16,2,192,128]{3,0,1,2:T(8,128)} copy(f32[16,2,192,128]{3,2,1,0:T(8,128)} %param.6) | data formatting | bytes 6291456 | tf_op args[1]
  16.3 31.2 %all-to-all-done = f32[16,2,192,128]{3,0,1,2:T(8,128)S(1)} async-done(((f32[16,2,192,128]{3,0,1,2:T(8,128)}), f32[16,2,192,128]{3,0,1,2:T(8,128)S(1)}, u32[]{:S(2)}, u32[]{:S(2)}) %all-to-all-start) | async-done | bytes 3145760 | tf_op jit(solution)/shard_map/all_to_all | solution.py:181
  47.5 4.7 %all-to-all-start.1 = ((f32[16,2,192,128]{3,0,1,2:T(8,128)}), f32[16,2,192,128]{3,0,1,2:T(8,128)}, u32[]{:S(2)}, u32[]{:S(2)}) async-start(f32[16,2,192,128]{3,0,1,2:T(8,128)} %copy.21), calls=%async_computation.1 | async-start | bytes 6291456 | tf_op jit(solution)/shard_map/all_to_all | solution.py:182
  59.2 28.8 %all-to-all-done.1 = f32[16,2,192,128]{3,0,1,2:T(8,128)} async-done(((f32[16,2,192,128]{3,0,1,2:T(8,128)}), f32[16,2,192,128]{3,0,1,2:T(8,128)}, u32[]{:S(2)}, u32[]{:S(2)}) %all-to-all-start.1) | async-done | bytes 3145760 | tf_op jit(solution)/shard_map/all_to_all | solution.py:182
  98.0 4.7 %collective-permute-start.1 = (f32[128,1,48,128]{3,2,1,0:T(8,128)}, f32[128,1,48,128]{3,2,1,0:T(8,128)}, u32[]{:S(2)}, u32[]{:S(2)}) collective-permute-start(f32[128,1,48,128]{3,2,1,0:T(8,128)} %get-tuple-element.32), channel_id=1, source_target_pairs={{4,0},{8,4},{12,8},{16,12},{20,16},{24,20},{28,24},{32,28},{36,32}... | collective-permute-start | bytes 9437192 | tf_op jit(solution)/shard_map/ppermute | solution.py:105
  106.9 5.4 %select_add_fusion = f32[2,192,128]{2,1,0:T(8,128)S(1)} fusion(s32[2,192,128]{2,1,0:T(8,128)S(1)} %copy-done.8, f32[]{:T(128)} %bitcast.14, f32[]{:T(128)} %bitcast.13, f32[]{:T(128)} %bitcast.12, f32[]{:T(128)} %bitcast.11, f32[]{:T(128)} %bitcast.10, f32[]{:T(128)} %bitcast.9, f32[]{:T(128)} %bitcast.8, f32[]{:T(128)} %bitcast.7), kind=kLoop, calls=%fused_computation.105 | loop fusion | flops 1130496 | bytes 393248 | tf_op jit(solution)/shard_map/add | solution.py:95
  118.7 21.0 %collective-permute-done = f32[1,50,128]{2,1,0:T(8,128)S(1)} collective-permute-done((f32[1,50,128]{2,1,0:T(8,128)S(1)}, f32[1,50,128]{2,1,0:T(8,128)S(1)}, u32[]{:S(2)}, u32[]{:S(2)}) %collective-permute-start) | collective-permute-done | bytes 25632 | tf_op jit(solution)/shard_map/ppermute | solution.py:22
  144.7 4.9 %collective-permute-start.5 = (f32[128,2,1,128]{3,2,1,0:T(1,128)}, f32[128,2,1,128]{3,2,1,0:T(1,128)}, u32[]{:S(2)}, u32[]{:S(2)}) collective-permute-start(f32[128,2,1,128]{3,2,1,0:T(1,128)} %get-tuple-element.36), channel_id=1, source_target_pairs={{0,1},{1,2},{2,3},{4,5},{5,6},{6,7},{8,9},{9,10},{10,11},{12,13},{... | collective-permute-start | bytes 393224 | tf_op jit(solution)/shard_map/ppermute | solution.py:104
  149.6 11.2 %fusion.97 = (f32[128,2,47,128]{3,2,1,0:T(8,128)}, f32[128,2,47,128]{3,2,1,0:T(8,128)}) fusion(f32[128,2,48,128]{3,2,1,0:T(8,128)} %copy-done), kind=kLoop, calls=%fused_computation.140 | loop fusion | bytes 24641536 | tf_op jit(solution)/shard_map/slice | solution.py:111
  160.9 19.9 %multiply_add_fusion.1 = (f32[128,2,48,128]{3,2,1,0:T(8,128)}, f32[128,2,48,128]{3,2,1,0:T(8,128)}) fusion(f32[128,2,48,128]{3,2,1,0:T(8,128)S(1)} %bitcast.32, f32[]{:T(128)S(6)} %div.53, f32[]{:T(128)S(6)} %mul.336, f32[]{:T(128)} %bitcast, f32[2,48,128]{2,1,0:T(8,128)S(1)} %get-tuple-element.42, f32[2,48,128]{2,1,0:T(8,128)S(1)} %get-tuple-element.45, ...), kind=kLoop, calls=%fused_computation.101 | loop fusion | flops 44040192 | bytes 50626572 | tf_op jit(solution)/shard_map/add | solution.py:162
  180.8 5.9 %fusion.93 = (f32[128,1,48,128]{3,2,1,0:T(8,128)}, f32[128,1,48,128]{3,2,1,0:T(8,128)}) fusion(f32[128,2,48,128]{3,2,1,0:T(8,128)} %get-tuple-element.7), kind=kLoop, calls=%fused_computation.136 | loop fusion | bytes 12582912 | tf_op jit(solution)/shard_map/slice | solution.py:111
  188.7 5.0 %collective-permute-start.7 = (f32[128,1,48,128]{3,2,1,0:T(8,128)}, f32[128,1,48,128]{3,2,1,0:T(8,128)}, u32[]{:S(2)}, u32[]{:S(2)}) collective-permute-start(f32[128,1,48,128]{3,2,1,0:T(8,128)} %get-tuple-element.25), channel_id=1, source_target_pairs={{0,4},{4,8},{8,12},{12,16},{16,20},{20,24},{24,28},{28,32},{32,36}... | collective-permute-start | bytes 9437192 | tf_op jit(solution)/shard_map/ppermute | solution.py:104
  198.9 4.9 %collective-permute-start.9 = (f32[128,2,1,128]{3,2,1,0:T(1,128)}, f32[128,2,1,128]{3,2,1,0:T(1,128)}, u32[]{:S(2)}, u32[]{:S(2)}) collective-permute-start(f32[128,2,1,128]{3,2,1,0:T(1,128)} %get-tuple-element.30), channel_id=1, source_target_pairs={{0,1},{1,2},{2,3},{4,5},{5,6},{6,7},{8,9},{9,10},{10,11},{12,13},{... | collective-permute-start | bytes 393224 | tf_op jit(solution)/shard_map/ppermute | solution.py:104
  203.8 11.2 %fusion.94 = (f32[128,2,47,128]{3,2,1,0:T(8,128)}, f32[128,2,47,128]{3,2,1,0:T(8,128)}) fusion(f32[128,2,48,128]{3,2,1,0:T(8,128)} %get-tuple-element.7), kind=kLoop, calls=%fused_computation.137 | loop fusion | bytes 24641536 | tf_op jit(solution)/shard_map/slice | solution.py:111
  215.0 11.9 %collective-permute-done.6 = f32[128,1,48,128]{3,2,1,0:T(8,128)} collective-permute-done((f32[128,1,48,128]{3,2,1,0:T(8,128)}, f32[128,1,48,128]{3,2,1,0:T(8,128)}, u32[]{:S(2)}, u32[]{:S(2)}) %collective-permute-start.6) | collective-permute-done | bytes 3145760 | tf_op jit(solution)/shard_map/ppermute | solution.py:105
  228.2 23.1 %broadcast_divide_fusion = (f32[128,2,48,128]{3,2,1,0:T(8,128)S(1)}, f32[128,2,48,128]{3,2,1,0:T(8,128)}) fusion(f32[]{:T(128)S(6)} %mul.380, f32[128,2,48,128]{3,2,1,0:T(8,128)} %get-tuple-element.8, f32[128,2,48,128]{3,2,1,0:T(8,128)} %get-tuple-element.7, f32[]{:T(128)} %bitcast, f32[2,48,128]{2,1,0:T(8,128)S(1)} %get-tuple-element.42, ...), kind=kLoop, calls=%fused_computation.103 | loop fusion | flops 47185920 | bytes 56918032 | tf_op jit(solution)/shard_map/div | solution.py:156
  266.8 4.9 %collective-permute-start.13 = (f32[128,2,1,128]{3,2,1,0:T(1,128)}, f32[128,2,1,128]{3,2,1,0:T(1,128)}, u32[]{:S(2)}, u32[]{:S(2)}) collective-permute-start(f32[128,2,1,128]{3,2,1,0:T(1,128)} %get-tuple-element.24), channel_id=1, source_target_pairs={{0,1},{1,2},{2,3},{4,5},{5,6},{6,7},{8,9},{9,10},{10,11},{12,13},{... | collective-permute-start | bytes 393224 | tf_op jit(solution)/shard_map/ppermute | solution.py:104
  271.7 11.4 %fusion.91 = (f32[128,2,47,128]{3,2,1,0:T(8,128)}, f32[128,2,47,128]{3,2,1,0:T(8,128)}) fusion(f32[128,2,48,128]{3,2,1,0:T(8,128)} %copy-done.3), kind=kLoop, calls=%fused_computation.134 | loop fusion | bytes 24641536 | tf_op jit(solution)/shard_map/slice | solution.py:111
  283.1 12.4 %collective-permute-done.10 = f32[128,1,48,128]{3,2,1,0:T(8,128)} collective-permute-done((f32[128,1,48,128]{3,2,1,0:T(8,128)}, f32[128,1,48,128]{3,2,1,0:T(8,128)}, u32[]{:S(2)}, u32[]{:S(2)}) %collective-permute-start.10) | collective-permute-done | bytes 3145760 | tf_op jit(solution)/shard_map/ppermute | solution.py:105
  296.7 15.5 %multiply_add_fusion = (f32[128,2,48,128]{3,2,1,0:T(8,128)S(1)}, f32[128,2,48,128]{3,2,1,0:T(8,128)}) fusion(f32[]{:T(128)S(6)} %div.61, f32[]{:T(128)S(6)} %mul.383, f32[128,2,48,128]{3,2,1,0:T(8,128)} %get-tuple-element.6, f32[]{:T(128)S(6)} %mul.380, f32[128,2,48,128]{3,2,1,0:T(8,128)S(1)} %bitcast.36, f32[]{:T(128)} %bitcast.16, ...), kind=kLoop, calls=%fused_computation.99 | loop fusion | flops 44040192 | bytes 50626576 | tf_op jit(solution)/shard_map/add | solution.py:162
  325.9 6.3 %multiply_bitcast_fusion = f32[1,128,2,48,128]{4,3,2,1,0:T(8,128)} fusion(f32[128,2,48,128]{3,2,1,0:T(8,128)} %get-tuple-element.6, f32[]{:T(128)S(6)} %sqrt.6), kind=kLoop, calls=%fused_computation.100 | loop fusion | flops 1572864 | bytes 12582916 | tf_op jit(solution)/shard_map/stack | solution.py:177
  339.0 6.3 %fusion.88 = (f32[128,2,47,128]{3,2,1,0:T(8,128)}, f32[128,2,47,128]{3,2,1,0:T(8,128)}) fusion(f32[128,2,48,128]{3,2,1,0:T(8,128)S(1)} %copy-done.2), kind=kLoop, calls=%fused_computation.131 | loop fusion | bytes 24641536 | tf_op jit(solution)/shard_map/slice | solution.py:112
  345.3 11.1 %collective-permute-done.14 = f32[128,1,48,128]{3,2,1,0:T(8,128)} collective-permute-done((f32[128,1,48,128]{3,2,1,0:T(8,128)}, f32[128,1,48,128]{3,2,1,0:T(8,128)}, u32[]{:S(2)}, u32[]{:S(2)}) %collective-permute-start.14) | collective-permute-done | bytes 3145760 | tf_op jit(solution)/shard_map/ppermute | solution.py:105
  357.6 15.1 %fusion.40 = f32[1,128,2,48,128]{4,3,2,1,0:T(8,128)S(1)} fusion(f32[128,2,48,128]{3,2,1,0:T(8,128)} %get-tuple-element.6, f32[128,2,48,128]{3,2,1,0:T(8,128)} %get-tuple-element.4, f32[128,2,48,128]{3,2,1,0:T(8,128)S(1)} %copy-done.2, f32[128,1,48,128]{3,2,1,0:T(8,128)} %collective-permute-done.14, f32[128,1,48,128]{3,2,1,0:T(8,128)} %get-tuple-element.17, ...), kind=kLoop, calls=%fused_computation.50 | loop fusion | flops 51904512 | bytes 50626584 | tf_op jit(solution)/shard_map/stack | solution.py:177
  372.7 5.2 %pad_maximum_fusion = (f32[2,64,2,48,128]{4,3,2,1,0:T(8,128)}, f32[2,64,2,48,128]{4,3,2,1,0:T(8,128)}) fusion(f32[1,128,2,48,128]{4,3,2,1,0:T(8,128)S(1)} %fusion.40, f32[1,128,2,48,128]{4,3,2,1,0:T(8,128)S(1)} %copy-done.6), kind=kLoop, calls=%fused_computation.53 | loop fusion | flops 3145728 | bytes 25165824 | tf_op jit(solution)/shard_map/stack | solution.py:177
  378.0 7.5 %dot_general.5 = f32[4,32,12288]{2,1,0:T(8,128)} reshape(f32[2,64,2,48,128]{4,3,2,1,0:T(8,128)} %get-tuple-element.11) | data formatting | bytes 12582912 | tf_op jit(solution)/shard_map/dot_general | solution.py:203
  385.5 7.4 %reshape.27 = f32[128,12288,1]{1,0,2:T(8,128)} reshape(f32[2,64,2,48,128]{4,3,2,1,0:T(8,128)} %get-tuple-element.12) | data formatting | bytes 12582912 | tf_op jit(solution)/shard_map/reshape | solution.py:201
  392.9 8.2 %convolution_bitcast_fusion = f32[4,128,32]{1,2,0:T(8,128)S(1)} fusion(f32[128,12288,1]{1,0,2:T(8,128)} %reshape.27, f32[4,32,12288]{2,1,0:T(8,128)} %dot_general.5), kind=kOutput, calls=%fused_computation.104 | convolution fusion | flops 2415919104 | bytes 12648448 | tf_op jit(solution)/shard_map/dot_general | solution.py:203
  401.1 6.8 %all_to_all.41 = f32[4,128,32]{1,2,0:T(8,128)S(1)} all-to-all(f32[4,128,32]{1,2,0:T(8,128)S(1)} %convolution_bitcast_fusion), channel_id=1, replica_groups=mesh['slab'=32,'col'=4] {'col'}, dimensions={0} | all-to-all | bytes 131072 | tf_op jit(solution)/shard_map/all_to_all | solution.py:217
  408.7 22.0 %shard_map.76 = f32[1,1,128]{2,1,0:T(1,128)} custom-call(f32[32,1,128]{2,1,0:T(1,128)} %bitcast.42), custom_call_target="tpu_custom_call" | custom-call | tf_op jit(solution)/shard_map/pallas_call | solution.py:78
  (87 shorter events, 73.4 us)
Async XLA Ops:
  6.0 41.5 %all-to-all-start = ((f32[16,2,192,128]{3,0,1,2:T(8,128)}), f32[16,2,192,128]{3,0,1,2:T(8,128)S(1)}, u32[]{:S(2)}, u32[]{:S(2)}) async-start(f32[16,2,192,128]{3,0,1,2:T(8,128)} %copy.19), calls=%async_computation | async-start | bytes 6291456 | tf_op jit(solution)/shard_map/all_to_all | solution.py:181
  10.9 41.3 %copy-start.9 = (f32[8]{0:T(128)S(1)}, f32[8]{0:T(128)}, u32[]{:S(2)}) copy-start(f32[8]{0:T(128)} %param.8) | copy-start | bytes 100
  10.9 42.6 %copy-start.10 = (s32[2]{0:T(128)S(1)}, s32[2]{0:T(128)}, u32[]{:S(2)}) copy-start(s32[2]{0:T(128)} %param.9) | copy-start | bytes 28
  47.5 7.9 %copy-start.7 = (f32[16,2,192,128]{3,0,1,2:T(8,128)}, f32[16,2,192,128]{3,0,1,2:T(8,128)S(1)}, u32[]{:S(2)}) copy-start(f32[16,2,192,128]{3,0,1,2:T(8,128)S(1)} %all-to-all-done) | copy-start | bytes 9437188
  47.5 40.5 %all-to-all-start.1 = ((f32[16,2,192,128]{3,0,1,2:T(8,128)}), f32[16,2,192,128]{3,0,1,2:T(8,128)}, u32[]{:S(2)}, u32[]{:S(2)}) async-start(f32[16,2,192,128]{3,0,1,2:T(8,128)} %copy.21), calls=%async_computation.1 | async-start | bytes 6291456 | tf_op jit(solution)/shard_map/all_to_all | solution.py:182
  59.2 33.2 %copy-start.4 = (f32[4,16,2,48,128]{4,3,2,1,0:T(8,128)}, f32[4,16,2,48,128]{4,3,2,1,0:T(8,128)S(1)}, u32[]{:S(2)}) copy-start(f32[4,16,2,48,128]{4,3,2,1,0:T(8,128)S(1)} %copy.20) | copy-start | bytes 9437188
  93.4 13.4 %copy-start.8 = (s32[2,192,128]{2,1,0:T(8,128)S(1)}, s32[2,192,128]{2,1,0:T(8,128)}, u32[]{:S(2)}) copy-start(s32[2,192,128]{2,1,0:T(8,128)} %param.7) | copy-start | bytes 589828
  98.0 62.9 %collective-permute-start.1 = (f32[128,1,48,128]{3,2,1,0:T(8,128)}, f32[128,1,48,128]{3,2,1,0:T(8,128)}, u32[]{:S(2)}, u32[]{:S(2)}) collective-permute-start(f32[128,1,48,128]{3,2,1,0:T(8,128)} %get-tuple-element.32), channel_id=1, source_target_pairs={{4,0},{8,4},{12,8},{16,12},{20,16},{24,20},{28,24},{32,28},{36,32}... | collective-permute-start | bytes 9437192 | tf_op jit(solution)/shard_map/ppermute | solution.py:105
  102.7 58.2 %collective-permute-start.3 = (f32[128,1,48,128]{3,2,1,0:T(8,128)}, f32[128,1,48,128]{3,2,1,0:T(8,128)}, u32[]{:S(2)}, u32[]{:S(2)}) collective-permute-start(f32[128,1,48,128]{3,2,1,0:T(8,128)} %get-tuple-element.31), channel_id=1, source_target_pairs={{0,4},{4,8},{8,12},{12,16},{16,20},{20,24},{24,28},{28,32},{32,36}... | collective-permute-start | bytes 9437192 | tf_op jit(solution)/shard_map/ppermute | solution.py:104
  112.3 27.4 %collective-permute-start = (f32[1,50,128]{2,1,0:T(8,128)S(1)}, f32[1,50,128]{2,1,0:T(8,128)S(1)}, u32[]{:S(2)}, u32[]{:S(2)}) collective-permute-start(f32[1,50,128]{2,1,0:T(8,128)S(1)} %get-tuple-element.40), channel_id=1, source_target_pairs={{4,0},{8,4},{12,8},{16,12},{20,16},{24,20},{28,24},{32,28},{36,32}... | collective-permute-start | bytes 76808 | tf_op jit(solution)/shard_map/ppermute | solution.py:22
  114.8 26.0 %collective-permute-start.2 = (f32[1,50,128]{2,1,0:T(8,128)S(1)}, f32[1,50,128]{2,1,0:T(8,128)S(1)}, u32[]{:S(2)}, u32[]{:S(2)}) collective-permute-start(f32[1,50,128]{2,1,0:T(8,128)S(1)} %get-tuple-element.39), channel_id=1, source_target_pairs={{0,4},{4,8},{8,12},{12,16},{16,20},{20,24},{24,28},{28,32},{32,36}... | collective-permute-start | bytes 76808 | tf_op jit(solution)/shard_map/ppermute | solution.py:19
  143.4 17.5 %collective-permute-start.4 = (f32[128,2,1,128]{3,2,1,0:T(1,128)}, f32[128,2,1,128]{3,2,1,0:T(1,128)S(1)}, u32[]{:S(2)}, u32[]{:S(2)}) collective-permute-start(f32[128,2,1,128]{3,2,1,0:T(1,128)} %get-tuple-element.35), channel_id=1, source_target_pairs={{1,0},{2,1},{3,2},{5,4},{6,5},{7,6},{9,8},{10,9},{11,10},{13,12},{... | collective-permute-start | bytes 393224 | tf_op jit(solution)/shard_map/ppermute | solution.py:105
  144.7 16.2 %slice-start = ((s8[6291456]{0:T(1024)(128)(4,1)}), s8[4194304]{0:T(1024)(128)(4,1)S(1)}, s32[]{:S(2)}) async-start(s8[6291456]{0:T(1024)(128)(4,1)} %bitcast.31), calls=%async_computation.3 | async-start | bytes 8388608
  144.7 16.2 %slice-start.1 = ((s8[6291456]{0:T(1024)(128)(4,1)}), s8[2097152]{0:T(1024)(128)(4,1)S(1)}, s32[]{:S(2)}) async-start(s8[6291456]{0:T(1024)(128)(4,1)} %bitcast.31), calls=%async_computation.4 | async-start | bytes 4194304
  144.7 16.2 %collective-permute-start.5 = (f32[128,2,1,128]{3,2,1,0:T(1,128)}, f32[128,2,1,128]{3,2,1,0:T(1,128)}, u32[]{:S(2)}, u32[]{:S(2)}) collective-permute-start(f32[128,2,1,128]{3,2,1,0:T(1,128)} %get-tuple-element.36), channel_id=1, source_target_pairs={{0,1},{1,2},{2,3},{4,5},{5,6},{6,7},{8,9},{9,10},{10,11},{12,13},{... | collective-permute-start | bytes 393224 | tf_op jit(solution)/shard_map/ppermute | solution.py:104
  186.8 40.2 %collective-permute-start.6 = (f32[128,1,48,128]{3,2,1,0:T(8,128)}, f32[128,1,48,128]{3,2,1,0:T(8,128)}, u32[]{:S(2)}, u32[]{:S(2)}) collective-permute-start(f32[128,1,48,128]{3,2,1,0:T(8,128)} %get-tuple-element.26), channel_id=1, source_target_pairs={{4,0},{8,4},{12,8},{16,12},{20,16},{24,20},{28,24},{32,28},{36,32}... | collective-permute-start | bytes 9437192 | tf_op jit(solution)/shard_map/ppermute | solution.py:105
  188.7 39.5 %collective-permute-start.7 = (f32[128,1,48,128]{3,2,1,0:T(8,128)}, f32[128,1,48,128]{3,2,1,0:T(8,128)}, u32[]{:S(2)}, u32[]{:S(2)}) collective-permute-start(f32[128,1,48,128]{3,2,1,0:T(8,128)} %get-tuple-element.25), channel_id=1, source_target_pairs={{0,4},{4,8},{8,12},{12,16},{16,20},{20,24},{24,28},{28,32},{32,36}... | collective-permute-start | bytes 9437192 | tf_op jit(solution)/shard_map/ppermute | solution.py:104
  197.6 17.5 %collective-permute-start.8 = (f32[128,2,1,128]{3,2,1,0:T(1,128)}, f32[128,2,1,128]{3,2,1,0:T(1,128)S(1)}, u32[]{:S(2)}, u32[]{:S(2)}) collective-permute-start(f32[128,2,1,128]{3,2,1,0:T(1,128)} %get-tuple-element.29), channel_id=1, source_target_pairs={{1,0},{2,1},{3,2},{5,4},{6,5},{7,6},{9,8},{10,9},{11,10},{13,12},{... | collective-permute-start | bytes 393224 | tf_op jit(solution)/shard_map/ppermute | solution.py:105
  198.9 29.3 %slice-start.2 = ((s8[6291456]{0:T(1024)(128)(4,1)}), s8[4194304]{0:T(1024)(128)(4,1)S(1)}, s32[]{:S(2)}) async-start(s8[6291456]{0:T(1024)(128)(4,1)} %bitcast.33), calls=%async_computation.5 | async-start | bytes 8388608
  198.9 29.3 %slice-start.3 = ((s8[6291456]{0:T(1024)(128)(4,1)}), s8[2097152]{0:T(1024)(128)(4,1)S(1)}, s32[]{:S(2)}) async-start(s8[6291456]{0:T(1024)(128)(4,1)} %bitcast.33), calls=%async_computation.6 | async-start | bytes 4194304
  198.9 16.2 %collective-permute-start.9 = (f32[128,2,1,128]{3,2,1,0:T(1,128)}, f32[128,2,1,128]{3,2,1,0:T(1,128)}, u32[]{:S(2)}, u32[]{:S(2)}) collective-permute-start(f32[128,2,1,128]{3,2,1,0:T(1,128)} %get-tuple-element.30), channel_id=1, source_target_pairs={{0,1},{1,2},{2,3},{4,5},{5,6},{6,7},{8,9},{9,10},{10,11},{12,13},{... | collective-permute-start | bytes 393224 | tf_op jit(solution)/shard_map/ppermute | solution.py:104
  255.9 39.6 %collective-permute-start.10 = (f32[128,1,48,128]{3,2,1,0:T(8,128)}, f32[128,1,48,128]{3,2,1,0:T(8,128)}, u32[]{:S(2)}, u32[]{:S(2)}) collective-permute-start(f32[128,1,48,128]{3,2,1,0:T(8,128)} %get-tuple-element.20), channel_id=1, source_target_pairs={{4,0},{8,4},{12,8},{16,12},{20,16},{24,20},{28,24},{32,28},{36,32}... | collective-permute-start | bytes 9437192 | tf_op jit(solution)/shard_map/ppermute | solution.py:105
  257.8 38.9 %collective-permute-start.11 = (f32[128,1,48,128]{3,2,1,0:T(8,128)}, f32[128,1,48,128]{3,2,1,0:T(8,128)}, u32[]{:S(2)}, u32[]{:S(2)}) collective-permute-start(f32[128,1,48,128]{3,2,1,0:T(8,128)} %get-tuple-element.19), channel_id=1, source_target_pairs={{0,4},{4,8},{8,12},{12,16},{16,20},{20,24},{24,28},{28,32},{32,36}... | collective-permute-start | bytes 9437192 | tf_op jit(solution)/shard_map/ppermute | solution.py:104
  265.5 17.6 %collective-permute-start.12 = (f32[128,2,1,128]{3,2,1,0:T(1,128)}, f32[128,2,1,128]{3,2,1,0:T(1,128)S(1)}, u32[]{:S(2)}, u32[]{:S(2)}) collective-permute-start(f32[128,2,1,128]{3,2,1,0:T(1,128)} %get-tuple-element.23), channel_id=1, source_target_pairs={{1,0},{2,1},{3,2},{5,4},{6,5},{7,6},{9,8},{10,9},{11,10},{13,12},{... | collective-permute-start | bytes 393224 | tf_op jit(solution)/shard_map/ppermute | solution.py:105
  266.8 29.9 %slice-start.4 = ((s8[6291456]{0:T(1024)(128)(4,1)}), s8[4194304]{0:T(1024)(128)(4,1)S(1)}, s32[]{:S(2)}) async-start(s8[6291456]{0:T(1024)(128)(4,1)} %bitcast.35), calls=%async_computation.7 | async-start | bytes 8388608
  266.8 29.9 %slice-start.5 = ((s8[6291456]{0:T(1024)(128)(4,1)}), s8[2097152]{0:T(1024)(128)(4,1)S(1)}, s32[]{:S(2)}) async-start(s8[6291456]{0:T(1024)(128)(4,1)} %bitcast.35), calls=%async_computation.8 | async-start | bytes 4194304
  266.8 16.3 %collective-permute-start.13 = (f32[128,2,1,128]{3,2,1,0:T(1,128)}, f32[128,2,1,128]{3,2,1,0:T(1,128)}, u32[]{:S(2)}, u32[]{:S(2)}) collective-permute-start(f32[128,2,1,128]{3,2,1,0:T(1,128)} %get-tuple-element.24), channel_id=1, source_target_pairs={{0,1},{1,2},{2,3},{4,5},{5,6},{6,7},{8,9},{9,10},{10,11},{12,13},{... | collective-permute-start | bytes 393224 | tf_op jit(solution)/shard_map/ppermute | solution.py:104
  316.8 39.6 %collective-permute-start.14 = (f32[128,1,48,128]{3,2,1,0:T(8,128)}, f32[128,1,48,128]{3,2,1,0:T(8,128)}, u32[]{:S(2)}, u32[]{:S(2)}) collective-permute-start(f32[128,1,48,128]{3,2,1,0:T(8,128)} %get-tuple-element.18), channel_id=1, source_target_pairs={{4,0},{8,4},{12,8},{16,12},{20,16},{24,20},{28,24},{32,28},{36,32}... | collective-permute-start | bytes 9437192 | tf_op jit(solution)/shard_map/ppermute | solution.py:105
  318.7 38.9 %collective-permute-start.15 = (f32[128,1,48,128]{3,2,1,0:T(8,128)}, f32[128,1,48,128]{3,2,1,0:T(8,128)}, u32[]{:S(2)}, u32[]{:S(2)}) collective-permute-start(f32[128,1,48,128]{3,2,1,0:T(8,128)} %get-tuple-element.17), channel_id=1, source_target_pairs={{0,4},{4,8},{8,12},{12,16},{16,20},{20,24},{24,28},{28,32},{32,36}... | collective-permute-start | bytes 9437192 | tf_op jit(solution)/shard_map/ppermute | solution.py:104
  333.1 12.2 %collective-permute-start.16 = (f32[128,2,1,128]{3,2,1,0:T(1,128)}, f32[128,2,1,128]{3,2,1,0:T(1,128)S(1)}, u32[]{:S(2)}, u32[]{:S(2)}) collective-permute-start(f32[128,2,1,128]{3,2,1,0:T(1,128)} %get-tuple-element.14), channel_id=1, source_target_pairs={{1,0},{2,1},{3,2},{5,4},{6,5},{7,6},{9,8},{10,9},{11,10},{13,12},{... | collective-permute-start | bytes 393224 | tf_op jit(solution)/shard_map/ppermute | solution.py:105
  334.4 10.9 %collective-permute-start.17 = (f32[128,2,1,128]{3,2,1,0:T(1,128)}, f32[128,2,1,128]{3,2,1,0:T(1,128)}, u32[]{:S(2)}, u32[]{:S(2)}) collective-permute-start(f32[128,2,1,128]{3,2,1,0:T(1,128)} %get-tuple-element.13), channel_id=1, source_target_pairs={{0,1},{1,2},{2,3},{4,5},{5,6},{6,7},{8,9},{9,10},{10,11},{12,13},{... | collective-permute-start | bytes 393224 | tf_op jit(solution)/shard_map/ppermute | solution.py:104
  357.6 15.1 %copy-start.6 = (f32[1,128,2,48,128]{4,3,2,1,0:T(8,128)S(1)}, f32[1,128,2,48,128]{4,3,2,1,0:T(8,128)}, u32[]{:S(2)}) copy-start(f32[1,128,2,48,128]{4,3,2,1,0:T(8,128)} %multiply_bitcast_fusion) | copy-start | bytes 18874372
  (5 other events, 21.8 us)
